TPU v7x, 512 devices: a whole 4x8x8 slice. The times are simulated.
512 devices in a mesh: ctx: 32 (over y, z_lo), head: 4 (over x), batch: 4 (over z_hi, core).
Axes of the slice: x: 4, y: 8, z: 8 (z_hi: 2, z_lo: 4; z = z_hi * 4 + z_lo), core: 2. Of those that a mesh axis runs over, the one named last changes fastest.
Arguments:
- queries: bfloat16 [4, 4096, 20, 128], P('batch', 'ctx', 'head'), may hold values from -64 to 64
- key_rows: bfloat16 [4, 4096, 4, 128], P('batch', 'ctx', 'head'), may hold values from -8 to 8
- block_order: int32 [64], replicated, may hold values from 0 to 63, each once
- conv_len: int32 [4], replicated, may hold values from 2048 to 4096
- gate_wq: float32 [128, 128], replicated, may hold values from -32 to 32
- gate_wk: float32 [384, 128], replicated, may hold values from -32 to 32
Outputs:
- teacher_map: float32 [4, 20, 64, 64], P('batch', 'head', 'ctx')
- grad_wq: float32 [128, 128], replicated
- grad_wk: float32 [384, 128], replicated
All inputs are finite; a program needn't handle non-finite values.
Results may differ from a plain program's by a relative error of at most 0.0003.
Values may be sent and summed in bfloat16 or wider, within the bound.
No kernel may reach another device: no remote copies, remote signals or barrier semaphores. Data moves between devices by JAX's collectives and lax.ppermute only.
A program may use at most 64 MiB of HBM per device.

v0:
```python
import math

import jax
import jax.numpy as jnp
from jax import lax
from jax.sharding import PartitionSpec as P

BLK = 64


masked_value = -1e30
norm_epsilon = 1e-06


def score_tile(query_group, key_tile, query_pos, key_pos, length):
    scores = jnp.einsum(
        "rgqd,kgd->gqrk", query_group, key_tile, preferred_element_type=jnp.float32
    ) / math.sqrt(key_tile.shape[-1])
    allowed = (key_pos[None, :] <= query_pos[:, None]) & (key_pos[None, :] < length)
    return (jnp.where(allowed, scores, masked_value), allowed)


def gate_loss(
    weight_query, weight_key, pooled_query, pooled_key, target_map, query_starts, key_starts, length
):
    kv_heads = pooled_key.shape[1]
    group_size = pooled_query.shape[1] // kv_heads
    width_gate = weight_query.shape[1]
    proj_query = jnp.einsum(
        "bhd,de->bhe", pooled_query, weight_query, precision=lax.Precision.HIGHEST
    )
    proj_key = jnp.einsum("bgd,de->bge", pooled_key, weight_key, precision=lax.Precision.HIGHEST)
    unit_query = proj_query * lax.rsqrt(
        jnp.mean(proj_query * proj_query, axis=-1, keepdims=True) + norm_epsilon
    )
    unit_key = proj_key * lax.rsqrt(
        jnp.mean(proj_key * proj_key, axis=-1, keepdims=True) + norm_epsilon
    )
    query_count = unit_query.shape[0]
    unit_query = unit_query.reshape(query_count, kv_heads, group_size, width_gate)
    logits = jnp.einsum(
        "igqe,jge->gqij", unit_query, unit_key, precision=lax.Precision.HIGHEST
    ) / math.sqrt(width_gate)
    logits = logits.reshape(kv_heads * group_size, query_count, unit_key.shape[0])
    allowed = (key_starts[None, :] <= query_starts[:, None]) & (key_starts[None, :] < length)
    weights_exp = jnp.where(allowed[None], jnp.exp(logits), 0.0)
    log_norm = jnp.log(jnp.sum(weights_exp, axis=-1, keepdims=True))
    positive = target_map > 0
    entropy_part = jnp.where(
        positive, target_map * jnp.log(jnp.where(positive, target_map, 1.0)), 0.0
    )
    divergence = entropy_part - target_map * (logits - log_norm)
    return jnp.sum(divergence)


def body(queries, key_rows, block_order, conv_len, gate_wq, gate_wk):
    tok_dev = queries.shape[1]
    head_dev = queries.shape[2]
    kv_dev = key_rows.shape[2]
    head_size = queries.shape[3]
    group_size = head_dev // kv_dev
    block_dev = tok_dev // BLK
    block_count = block_order.shape[0]
    ctx_index = lax.axis_index("ctx")
    length = lax.dynamic_index_in_dim(conv_len, lax.axis_index("batch"), keepdims=False)
    own_blocks = lax.dynamic_slice_in_dim(block_order, ctx_index * block_dev, block_dev)
    offsets = jnp.arange(BLK, dtype=jnp.int32)
    query_pos = (own_blocks[:, None] * BLK + offsets[None, :]).reshape(tok_dev)
    valid_row = (query_pos < length)[:, None]
    query_group = queries[0].reshape(tok_dev, kv_dev, group_size, head_size)

    def tile_loop(update, carry, segment):
        width_keys = segment.shape[1]
        sub_rows = math.gcd(width_keys, 512)
        key_pos = (block_order[:, None] * BLK + offsets[None, :]).reshape(width_keys)

        def advance(step_index, state):
            first = step_index * sub_rows
            key_tile = lax.dynamic_slice_in_dim(segment[0], first, sub_rows, 0)
            tile_pos = lax.dynamic_slice_in_dim(key_pos, first, sub_rows, 0)
            column = first // BLK
            result = update(state, key_tile, tile_pos, column)
            return result

        return lax.fori_loop(0, width_keys // sub_rows, advance, carry)

    def merge_stats(highest, summed, masked, allowed):
        new_high = jnp.maximum(highest, jnp.max(masked, axis=-1))
        fresh = jnp.sum(jnp.where(allowed, jnp.exp(masked - new_high[..., None]), 0.0), axis=-1)
        return (new_high, summed * jnp.exp(highest - new_high) + fresh)

    stats_shape = (kv_dev, group_size, tok_dev)
    start_high = jnp.full(stats_shape, masked_value, jnp.float32)
    start_sum = jnp.zeros(stats_shape, jnp.float32)

    def add_stats(state, key_tile, tile_pos, column):
        masked, allowed = score_tile(query_group, key_tile, query_pos, tile_pos, length)
        return merge_stats(state[0], state[1], masked, allowed)

    highest, summed = tile_loop(
        add_stats, (start_high, start_sum), lax.all_gather(key_rows, "ctx", axis=1, tiled=True)
    )
    log_total = highest + jnp.log(summed)

    def add_pool(state, key_tile, tile_pos, column):
        masked, allowed = score_tile(query_group, key_tile, query_pos, tile_pos, length)
        probs = jnp.where(valid_row, jnp.exp(masked - log_total[..., None]), 0.0)
        tile_max = probs.reshape(
            kv_dev, group_size, block_dev, BLK, key_tile.shape[0] // BLK, BLK
        ).max(axis=(3, 5))
        return lax.dynamic_update_slice_in_dim(state, tile_max, column, 3)

    start_pool = jnp.zeros((kv_dev, group_size, block_dev, block_count), jnp.float32)
    pooled = tile_loop(add_pool, start_pool, lax.all_gather(key_rows, "ctx", axis=1, tiled=True))
    pooled = pooled.reshape(head_dev, block_dev, block_count)
    query_starts = own_blocks * BLK
    valid_block = (query_starts < length)[None, :, None]
    totals = jnp.sum(pooled, axis=-1, keepdims=True)
    target = jnp.where(valid_block, pooled / jnp.where(valid_block, totals, 1.0), 0.0)
    key_local = key_rows[0].reshape(block_dev, BLK, kv_dev, head_size)
    pooled_local = jnp.concatenate(
        [
            jnp.max(key_local, axis=1).astype(jnp.float32),
            jnp.min(key_local, axis=1).astype(jnp.float32),
            jnp.mean(key_local, axis=1, dtype=jnp.float32),
        ],
        axis=-1,
    )
    pooled_all = lax.all_gather(pooled_local, "ctx", axis=0, tiled=True)
    pooled_query = jnp.mean(
        queries[0].reshape(block_dev, BLK, head_dev, head_size), axis=1, dtype=jnp.float32
    )
    key_starts = block_order * BLK

    def local_loss(weight_query, weight_key):
        return gate_loss(
            weight_query,
            weight_key,
            pooled_query,
            pooled_all,
            target,
            query_starts,
            key_starts,
            length,
        )

    loss_value, pullback = jax.vjp(local_loss, gate_wq, gate_wk)
    grad_query, grad_key = pullback(jnp.ones((), jnp.float32))
    grad_query, grad_key = lax.psum((grad_query, grad_key), ("ctx", "head", "batch"))
    return (target[None], grad_query, grad_key)


def solution(mesh):
    in_specs = (
        P("batch", "ctx", "head", None),
        P("batch", "ctx", "head", None),
        P(),
        P(),
        P(),
        P(),
    )
    out_specs = (P("batch", "head", "ctx", None), P(), P())
    return jax.shard_map(body, mesh=mesh, in_specs=in_specs, out_specs=out_specs, check_vma=False)
```

profile of v0, /device:TPU:1, one launch (start us, length us, event | category | flops | bytes accessed | tf_op | source)
XLA Modules:
  0.0 550.3 jit_solution(3898082681139945655)
XLA Ops:
  8.0 0.8 fusion.68
  8.8 0.8 convert_reduce_fusion.1
  10.4 70.3 %all_gather.8 = f32[64,1,384]{2,1,0:T(1,128)S(1)} all-gather(f32[2,1,384]{2,1,0:T(1,128)S(1)} %pad_maximum_fusion), channel_id=1, replica_groups=mesh['ctx'=32,'head'=4,'batch'=4] {'ctx'}, dimensions={0}, use_global_device_ids=true | all-gather | bytes 101376 | tf_op jit(solution)/shard_map/all_gather | solution.py:129
  80.7 1.2 dynamic_slice.35
  81.9 1.4 broadcast_compare_fusion.4
  83.3 1.0 convert_reduce_fusion
  84.2 1.3 broadcast_compare_fusion.3
  85.9 1.1 multiply_reduce_fusion.3
  87.4 59.0 %all-gather.2.cloned.1.call-done = bf16[1,4096,1,128]{3,1,2,0:T(8,128)(2,1)} async-done(((bf16[1,128,1,128]{3,1,2,0:T(8,128)(2,1)}), bf16[1,4096,1,128]{3,1,2,0:T(8,128)(2,1)}) %all-gather.2.cloned.1.call-update) | async-done | bytes 1048592 | tf_op jit(solution)/shard_map/all_gather | solution.py:114
  146.4 22.0 %while.33 = (s32[]{:T(128)}, f32[1,5,128]{2,1,0:T(8,128)S(1)}, f32[1,5,128]{2,1,0:T(8,128)S(1)}, s32[4096]{0:T(1024)S(1)}, s32[]{:T(128)}, /*index=5*/bf16[1,409...) while((s32[]{:T(128)}, f32[1,5,128]{2,1,0:T(8,128)S(1)}, ...), condition=%wide.region_3.4_spmd.clone, body=%wide.region_0.3_spmd.clone.sunk | while | flops 85987080 | bytes 3155650 | solution.py:85
  147.5 1.3 fusion.74
  149.2 0.7 broadcast_compare_fusion.8
  150.3 1.3 fusion.74
  151.9 0.7 broadcast_compare_fusion.8
  153.0 1.3 fusion.74
  154.7 0.7 broadcast_compare_fusion.8
  155.8 1.3 fusion.74
  157.4 0.7 broadcast_compare_fusion.8
  158.5 1.3 fusion.74
  160.2 0.7 broadcast_compare_fusion.8
  161.3 1.3 fusion.74
  162.9 0.7 broadcast_compare_fusion.8
  164.0 1.3 fusion.74
  165.7 0.7 broadcast_compare_fusion.8
  166.8 1.3 fusion.74
  168.5 74.3 %while.34 = (s32[]{:T(128)}, f32[1,5,2,64]{3,2,1,0:T(2,128)S(1)}, s32[4096]{0:T(1024)S(1)}, s32[]{:T(128)}, bf16[1,4096,1,128]{3,1,2,0:T(8,128)(2,1)}, /*index=5...) while((s32[]{:T(128)}, f32[1,5,2,64]{3,2,1,0:T(2,128)S(1)}, ...), condition=%wide.region_6.7_spmd.clone.clone, body=%wide.region_4.6_spmd.clone.clone.sunk | while | flops 85656376 | bytes 5683170 | solution.py:85
  170.4 2.5 exponential_select_fusion.2
  172.9 2.8 reshape.363
  175.7 1.1 reduce_max.47
  179.1 2.5 exponential_select_fusion.2
  181.6 2.8 reshape.363
  184.4 1.1 reduce_max.47
  185.7 0.9 dynamic_update_slice.13
  186.6 0.7 broadcast_compare_fusion.9
  188.5 2.5 exponential_select_fusion.2
  191.0 2.8 reshape.363
  193.8 1.1 reduce_max.47
  195.0 0.9 dynamic_update_slice.13
  197.8 2.5 exponential_select_fusion.2
  200.4 2.8 reshape.363
  203.2 1.1 reduce_max.47
  204.4 0.9 dynamic_update_slice.13
  207.2 2.5 exponential_select_fusion.2
  209.7 2.8 reshape.363
  212.6 1.1 reduce_max.47
  213.8 0.9 dynamic_update_slice.13
  214.7 0.7 broadcast_compare_fusion.9
  216.6 2.5 exponential_select_fusion.2
  219.1 2.8 reshape.363
  221.9 1.1 reduce_max.47
  223.2 0.9 dynamic_update_slice.13
  226.0 2.5 exponential_select_fusion.2
  228.5 2.8 reshape.363
  231.3 1.1 reduce_max.47
  232.5 0.9 dynamic_update_slice.13
  235.3 2.5 exponential_select_fusion.2
  237.9 2.8 reshape.363
  240.7 1.1 reduce_max.47
  241.9 0.9 dynamic_update_slice.13
  244.0 1.2 fusion.18
  245.2 0.9 convolution_bitcast_fusion
  246.8 293.5 %all-reduce.3.cloned.1.call-done = (f32[128,128]{1,0:T(8,128)}, f32[384,128]{1,0:T(8,128)}) async-done(((f32[128,128]{1,0:T(8,128)}, f32[384,128]{1,0:T(8,128)}), (f32[128,128]{1,0:T(8,128)}, f32[384,128]{1,0:T(8,128)})) %all-reduce.3.cloned.1.call-update) | async-done | bytes 262160 | tf_op jit(solution)/shard_map/psum | solution.py:149
  540.3 1.5 copy.90
  541.8 1.6 copy.91
  (146 shorter events, 24.6 us)
Async XLA Ops:
  7.2 78.4 %copy-start = (f32[384,128]{1,0:T(8,128)S(1)}, f32[384,128]{1,0:T(8,128)}, u32[]{:S(2)}) copy-start(f32[384,128]{1,0:T(8,128)} %param.15) | copy-start | bytes 589828
  7.2 139.3 %all-gather.2.cloned.1.call-start = ((), (), s32[]{:S(2)}) async-start(), calls=%async_computation | async-start | bytes 1081344 | tf_op jit(solution)/shard_map/all_gather | solution.py:114
  7.9 532.4 %all-reduce.3.cloned.1.call-start = ((), (), s32[]{:S(2)}) async-start(), calls=%async_computation.1 | async-start | bytes 524288 | tf_op jit(solution)/shard_map/psum | solution.py:149
Sparse Core Ops, SparseCore 0:
  10.1 136.3 all-gather.1
  246.3 294.0 all-reduce.2
where the time goes:
time: 552 us; the launch traced here: 550 us
  waiting for transfers between devices  353 us (64%)
  blocking collectives  70.3 us (13%)
  other arithmetic  39.2 us (7%)
  local copies, waits for them, and re-layouts  36.8 us (7%)
  matrix products  35.6 us (6%)
  between operations  14.1 us (3%)
    psum x1, waiting for transfers between devices, body(): lax.psum((grad_query, grad_key), ('ctx', 'head', 'batch'))  294 us
    all_gather x1, blocking collectives, body(): pooled_all = lax.all_gather(pooled_local, 'ctx', axis=0, tiled=True)  70.3 us
    all_gather x1, waiting for transfers between devices, body(): lax.all_gather(key_rows, 'ctx', axis=1, tiled=True)  59 us
    dot_general x16, matrix products, score_tile(): jnp.einsum('rgqd,kgd->gqrk', query_group, key_tile, preferred_element_typ...  30.9 us
    reshape x8, local copies, waits for them, and re-layouts, add_pool(): probs.reshape(kv_dev, group_size, block_dev, BLK, key_tile.shape[0] // BL...  22.6 us
    lt x16, other arithmetic, score_tile(): key_pos[None, :] < length  11.6 us
  transfers between devices with their start and end apart: 2, of which 2 were waited for; matrix products, arithmetic and copies ran while one was open for 2% of the time, Pallas kernels for 0%

commit v1 on v0

v1 whole, which is shorter than its diff:
```python
import functools
import math

import jax
import jax.numpy as jnp
from jax import lax
from jax.experimental import pallas as pl
from jax.experimental.pallas import tpu as pltpu
from jax.sharding import Mesh
from jax.sharding import PartitionSpec as P

BLK = 64
LANES = 128
MASKED = -1e30
EPS = 1e-06
FAR = 1 << 20
HIGHEST = lax.Precision.HIGHEST

CTX = ("y", "zl")
SCATTER = ("c", "x", "y")
REST = ("zh", "zl")


def dot(a, b, dims):
    return lax.dot_general(
        a, b, (dims, ((), ())), precision=HIGHEST, preferred_element_type=jnp.float32
    )


def kernel(group, blocks, scal, order, q_ref, k_ref, ordv, wq, wk, t_ref, g_ref, m_ref, pk_ref):
    rows = q_ref.shape[0]
    dim = q_ref.shape[1]
    toks = rows // group
    own = toks // BLK
    length = scal[0]
    qb = [scal[1 + i] for i in range(own)]
    tok = lax.rem(lax.broadcasted_iota(jnp.int32, (1, rows), 1), toks)
    pos = lax.rem(tok, BLK)
    part = tok // BLK
    start = jnp.zeros_like(tok)
    for i in range(own):
        start = jnp.where(part == i, qb[i] * BLK, start)
    pos = pos + start
    limit = jnp.minimum(pos, length - 1)
    sub = lax.broadcasted_iota(jnp.int32, (BLK, rows), 0)
    scale = math.log2(math.e) / math.sqrt(dim)
    step = 8
    width = step * BLK
    q = q_ref[...]
    m_ref[...] = jnp.full(m_ref.shape, MASKED, jnp.float32)
    pk_ref[...] = jnp.zeros(pk_ref.shape, jnp.float32)

    def chunk(c, carry):
        high, total = carry
        k = k_ref[pl.ds(pl.multiple_of(c * width, width), width), :]
        s = lax.dot_general(k, q, (((1,), (1,)), ((), ())), preferred_element_type=jnp.float32)
        kf = k.astype(jnp.float32).reshape(step, BLK, dim)
        at = pl.ds(pl.multiple_of(c * step, step), step)
        pk_ref[at, 0:dim] = jnp.max(kf, axis=1)
        pk_ref[at, dim : 2 * dim] = jnp.min(kf, axis=1)
        pk_ref[at, 2 * dim : 3 * dim] = jnp.sum(kf, axis=1) * (1.0 / BLK)
        tiles = []
        tops = []
        for j in range(step):
            ok = sub <= limit - order[c * step + j] * BLK
            tile = jnp.where(ok, s[j * BLK : (j + 1) * BLK] * scale, MASKED)
            tiles.append(tile)
            tops.append(jnp.max(tile, axis=0, keepdims=True))
        top = jnp.concatenate(tops, axis=0)
        m_ref[at, :] = top
        new = jnp.maximum(high, jnp.max(top, axis=0, keepdims=True))
        fresh = jnp.zeros((8, rows), jnp.float32)
        for j in range(step):
            e = jnp.exp2(tiles[j] - new)
            fresh = fresh + jnp.sum(e.reshape(BLK // 8, 8, rows), axis=0)
        total = total * jnp.exp2(high - new) + fresh
        return new, total

    high, total = lax.fori_loop(
        0,
        blocks // step,
        chunk,
        (jnp.full((1, rows), MASKED, jnp.float32), jnp.zeros((8, rows), jnp.float32)),
    )
    log_total = high + jnp.log2(jnp.sum(total, axis=0, keepdims=True))
    depth = jnp.where(pos < length, m_ref[...] - log_total, MASKED)
    depth = jnp.max(jnp.transpose(depth).reshape(group * own, BLK, LANES), axis=1)
    count = t_ref.shape[0]
    pad = count - group * own
    depth = jnp.concatenate([depth, jnp.full((pad, LANES), MASKED, jnp.float32)], axis=0)
    pooled = jnp.exp2(depth)
    row = lax.broadcasted_iota(jnp.int32, (count, 1), 0)
    qstart = jnp.zeros((count, 1), jnp.int32)
    for i in range(own):
        qstart = jnp.where(lax.rem(row, own) == i, qb[i] * BLK, qstart)
    good = (qstart < length) & (row < group * own)
    totals = jnp.sum(pooled, axis=1, keepdims=True)
    target = jnp.where(good, pooled / jnp.where(good, totals, 1.0), 0.0)
    t_ref[...] = target

    pq = jnp.sum(q.astype(jnp.float32).reshape(group * own, BLK, dim), axis=1) * (1.0 / BLK)
    pq = jnp.concatenate([pq, jnp.zeros((pad, dim), jnp.float32)], axis=0)
    pk = pk_ref[...]
    xq = dot(pq, wq[...], ((1,), (0,)))
    xk = dot(pk, wk[...], ((1,), (0,)))
    width_gate = xq.shape[1]
    rq = lax.rsqrt(jnp.mean(xq * xq, axis=1, keepdims=True) + EPS)
    rk = lax.rsqrt(jnp.mean(xk * xk, axis=1, keepdims=True) + EPS)
    uq = xq * rq
    uk = xk * rk
    gate_scale = 1.0 / math.sqrt(width_gate)
    logits = dot(uq, uk, ((1,), (1,))) * gate_scale
    kstart = ordv[...] * BLK
    allowed = (kstart <= qstart) & (kstart < length)
    weights = jnp.where(allowed, jnp.exp(logits), 0.0)
    soft = weights / jnp.sum(weights, axis=1, keepdims=True)
    dl = (soft * jnp.sum(target, axis=1, keepdims=True) - target) * gate_scale
    duq = dot(dl, uk, ((1,), (0,)))
    duk = dot(dl, uq, ((0,), (0,)))
    dxq = rq * (duq - uq * jnp.mean(duq * uq, axis=1, keepdims=True))
    dxk = rk * (duk - uk * jnp.mean(duk * uk, axis=1, keepdims=True))
    g_ref[0:dim, :] = dot(pq, dxq, ((0,), (0,)))
    g_ref[dim : 4 * dim, :] = dot(pk, dxk, ((0,), (0,)))


def body(queries, key_rows, block_order, conv_len, gate_wq, gate_wk):
    toks = queries.shape[1]
    group = queries.shape[2]
    dim = queries.shape[3]
    own = toks // BLK
    blocks = block_order.shape[0]
    ctx = lax.axis_size(CTX)
    keys = lax.all_to_all(
        jnp.broadcast_to(key_rows[0, :, 0, :][None], (ctx, toks, dim)), CTX, 0, 0, tiled=True
    ).reshape(ctx * toks, dim)
    length = lax.dynamic_index_in_dim(conv_len, lax.axis_index(("zh", "c")))
    mine = lax.dynamic_slice_in_dim(block_order, lax.axis_index(CTX) * own, own)
    scal = jnp.concatenate([length, mine])
    q = jnp.transpose(queries[0], (1, 0, 2)).reshape(group * toks, dim)
    ordv = jnp.concatenate([block_order, jnp.full((LANES - blocks,), FAR, jnp.int32)])[None]
    count = 16
    width = gate_wq.shape[1]
    smem = pl.BlockSpec(memory_space=pltpu.SMEM)
    vmem = pl.BlockSpec(memory_space=pltpu.VMEM)
    target, grads = pl.pallas_call(
        functools.partial(kernel, group, blocks),
        out_shape=(
            jax.ShapeDtypeStruct((count, LANES), jnp.float32),
            jax.ShapeDtypeStruct((4 * dim, width), jnp.float32),
        ),
        in_specs=[smem, smem, vmem, vmem, vmem, vmem, vmem],
        out_specs=(vmem, vmem),
        scratch_shapes=[
            pltpu.VMEM((LANES, group * toks), jnp.float32),
            pltpu.VMEM((LANES, 3 * dim), jnp.float32),
        ],
        name="teacher_gate",
    )(scal, block_order, q, keys, ordv, gate_wq, gate_wk)

    parts = lax.axis_size(SCATTER)
    rest = lax.axis_size(REST)
    piece = 4 * dim // parts
    mineg = lax.all_to_all(grads.reshape(parts, piece, width), SCATTER, 0, 0, tiled=True)
    mineg = jnp.sum(mineg, axis=0)
    mineg = lax.all_to_all(
        jnp.broadcast_to(mineg[None], (rest, piece, width)), REST, 0, 0, tiled=True
    )
    mineg = jnp.sum(mineg, axis=0)
    grads = lax.all_to_all(
        jnp.broadcast_to(mineg[None], (parts, piece, width)), SCATTER, 0, 0, tiled=True
    ).reshape(4 * dim, width)
    target = target[: group * own, :blocks].reshape(1, group, own, blocks)
    return target, grads[:dim], grads[dim:]


def solution(mesh):
    fine = Mesh(mesh.devices.reshape(8, 4, 4, 2, 2), ("y", "zl", "x", "zh", "c"))
    rows = P(("zh", "c"), CTX, "x", None)
    return jax.shard_map(
        body,
        mesh=fine,
        in_specs=(rows, rows, P(), P(), P(), P()),
        out_specs=(P(("zh", "c"), "x", CTX, None), P(), P()),
        check_vma=False,
    )
```

time: 552 us -> 113 us (0.20)
  waiting for transfers between devices: 353 us -> 36 us
  other arithmetic: 39.2 us -> 1.31 us
  matrix products: 35.6 us -> 0 us
  blocking collectives: 70.3 us -> 37.3 us
  local copies, waits for them, and re-layouts: 36.8 us -> 8.08 us
  starting transfers between devices: 0.08 us -> 20.5 us
  between operations: 14.1 us -> 0.68 us
  Pallas kernels: 0 us -> 8.57 us
    psum x1 -> x0, waiting for transfers between devices: 294 us -> none  [body(): lax.psum((grad_query, grad_key), ('ctx', 'head', 'batch'))]
    all_gather x1 -> x0, blocking collectives: 70.3 us -> none  [body(): pooled_all = lax.all_gather(pooled_local, 'ctx', axis=0, tiled=True)]
    all_gather x1 -> x0, waiting for transfers between devices: 59 us -> none  [body(): lax.all_gather(key_rows, 'ctx', axis=1, tiled=True)]
    all_to_all x0 -> x2, blocking collectives: none -> 37.3 us  [the longest x1 23.3 us: body(): lax.all_to_all(grads.reshape(parts, piece, width), SCATTER, 0, 0, tiled=T...]
    all_to_all x0 -> x2, waiting for transfers between devices: none -> 36 us  [the longest x1 23.2 us: body(): lax.all_to_all(jnp.broadcast_to(key_rows[0, :, 0, :][None], (ctx, toks, d...]
    dot_general x23 -> x0, matrix products: 35.6 us -> none  [the longest x16 30.9 us: score_tile(): jnp.einsum('rgqd,kgd->gqrk', query_group, key_tile, preferred_element_typ...]
    reshape x8 -> x1, local copies, waits for them, and re-layouts: 22.6 us -> 0.6 us  [body(): target = target[:group * own, :blocks].reshape(1, group, own, blocks)]
    all_to_all x0 -> x2, starting transfers between devices: none -> 20.5 us  [the longest x1 13.5 us: body(): lax.all_to_all(jnp.broadcast_to(key_rows[0, :, 0, :][None], (ctx, toks, d...]
  transfers between devices with their start and end apart: 2 -> 2, of which waited for: 2 -> 2; matrix products, arithmetic and copies ran while one was open for 2% -> 3% of each run, Pallas kernels for 0% -> 0%
where the time goes in v1:
time: 113 us; the launch traced here: 112 us
  blocking collectives  37.3 us (33%)
  waiting for transfers between devices  36 us (32%)
  starting transfers between devices  20.5 us (18%)
  Pallas kernels  8.57 us (8%)
  local copies, waits for them, and re-layouts  8.08 us (7%)
  other arithmetic  1.31 us (1%)
    all_to_all x1, blocking collectives, body(): lax.all_to_all(grads.reshape(parts, piece, width), SCATTER, 0, 0, tiled=T...  23.3 us
    all_to_all x1, waiting for transfers between devices, body(): lax.all_to_all(jnp.broadcast_to(key_rows[0, :, 0, :][None], (ctx, toks, d...  23.2 us
    all_to_all x1, blocking collectives, body(): lax.all_to_all(jnp.broadcast_to(mineg[None], (rest, piece, width)), REST,...  14.1 us
    all_to_all x1, starting transfers between devices, body(): lax.all_to_all(jnp.broadcast_to(key_rows[0, :, 0, :][None], (ctx, toks, d...  13.5 us
    all_to_all x1, waiting for transfers between devices, body(): lax.all_to_all(jnp.broadcast_to(mineg[None], (parts, piece, width)), SCAT...  12.8 us
    pallas_call x1, Pallas kernels, body(): pl.pallas_call(functools.partial(kernel, group, blocks), out_shape=(jax.S...  8.57 us
    all_to_all x1, starting transfers between devices, body(): lax.all_to_all(jnp.broadcast_to(mineg[None], (parts, piece, width)), SCAT...  7.03 us
    unnamed x8, local copies, waits for them, and re-layouts  2.28 us
  transfers between devices with their start and end apart: 2, of which 2 were waited for; matrix products, arithmetic and copies ran while one was open for 3% of the time, Pallas kernels for 0%

profile of v1, /device:TPU:1, one launch (start us, length us, event | category | flops | bytes accessed | tf_op | source)
XLA Modules:
  0.0 112.4 jit_solution(6304570044611101172)
XLA Ops:
  0.6 2.0 %broadcast_in_dim.11 = bf16[32,128,128]{2,1,0:T(8,128)(2,1)} broadcast(bf16[128,128]{1,0:T(8,128)(2,1)} %bitcast.18), dimensions={1,2} | broadcast | bytes 1081344 | tf_op jit(solution)/shard_map/broadcast_in_dim | solution.py:134
  2.6 13.5 %all-to-all-start = ((bf16[32,128,128]{2,1,0:T(8,128)(2,1)}), bf16[32,128,128]{2,1,0:T(8,128)(2,1)S(1)}, u32[]{:S(2)}, u32[]{:S(2)}) async-start(bf16[32,128,128]{2,1,0:T(8,128)(2,1)} %broadcast_in_dim.11), calls=%async_computation | async-start | bytes 2097152 | tf_op jit(solution)/shard_map/all_to_all | solution.py:133
  16.1 0.0 copy-start.3
  16.1 0.6 copy-done.3
  16.7 0.6 dynamic_slice.7
  17.3 0.0 copy-start.2
  17.3 0.7 copy-done.2
  18.0 0.1 dynamic_slice.8
  18.0 0.5 pad_bitcast_fusion.ordv
  18.6 1.2 %pad_add_fusion.scal = s32[3]{0:T(128)} fusion(s32[2]{0:T(128)S(1)} %dynamic_slice.8, s32[1]{0:T(128)} %dynamic_slice.7), kind=kLoop, calls=%fused_computation.2 | loop fusion | flops 3 | bytes 24 | tf_op jit(solution)/shard_map/concatenate | solution.py:138
  19.8 23.2 %all-to-all-done = bf16[32,128,128]{2,1,0:T(8,128)(2,1)S(1)} async-done(((bf16[32,128,128]{2,1,0:T(8,128)(2,1)}), bf16[32,128,128]{2,1,0:T(8,128)(2,1)S(1)}, u32[]{:S(2)}, u32[]{:S(2)}) %all-to-all-start) | async-done | bytes 1048608 | tf_op jit(solution)/shard_map/all_to_all | solution.py:133
  43.0 0.0 copy-start
  43.0 1.0 copy-done
  44.0 8.6 %teacher_gate.1 = (f32[16,128]{1,0:T(8,128)}, f32[512,128]{1,0:T(8,128)}) custom-call(s32[3]{0:T(128)} %pad_add_fusion.scal, s32[64]{0:T(128)} %order.1, bf16[640,128]{1,0:T(8,128)(2,1)} %bitcast.17, bf16[4096,128]{1,0:T(8,128)(2,1)} %bitcast.15, s32[1,128]{1,0:T(1,128)} %pad_bitcast_fusion.ordv, f32[128,128]{1,0:T(8,128)} %wq.1, f32[384,128]{1,0:T(8,128)} %wk.1), custom_call_target="tpu_custom_call" | custom-call | tf_op jit(solution)/shard_map/teacher_gate/pallas_call | solution.py:145
  52.5 23.3 %all_to_all.20 = f32[64,8,128]{2,1,0:T(8,128)S(1)} all-to-all(f32[64,8,128]{2,1,0:T(8,128)} %bitcast.16), channel_id=1, replica_groups=mesh['y'=8,'zl'=4,'x'=4,'zh'=2,'c'=2] {'c','x','y'}, dimensions={0} | all-to-all | bytes 524288 | tf_op jit(solution)/shard_map/all_to_all | solution.py:163
  75.8 0.1 reduce_sum.18
  75.9 14.1 %all_to_all.21 = f32[8,8,128]{2,1,0:T(8,128)S(1)} all-to-all(f32[8,8,128]{2,1,0:T(8,128)S(1)} %broadcast_in_dim.26), channel_id=1, replica_groups=mesh['y'=8,'zl'=4,'x'=4,'zh'=2,'c'=2] {'zh','zl'}, dimensions={0} | all-to-all | bytes 65536 | tf_op jit(solution)/shard_map/all_to_all | solution.py:165
  90.0 0.7 broadcast_in_dim.27
  90.7 0.0 copy-start.1
  90.7 7.0 %all-to-all-start.3 = ((f32[64,8,128]{2,1,0:T(8,128)}), f32[64,8,128]{2,1,0:T(8,128)S(1)}, u32[]{:S(2)}, u32[]{:S(2)}) async-start(f32[64,8,128]{2,1,0:T(8,128)} %broadcast_in_dim.27), calls=%async_computation.3 | async-start | bytes 524288 | tf_op jit(solution)/shard_map/all_to_all | solution.py:169
  97.7 0.0 copy-done.1
  97.7 0.6 reshape.26
  98.3 12.8 %all-to-all-done.3 = f32[64,8,128]{2,1,0:T(8,128)S(1)} async-done(((f32[64,8,128]{2,1,0:T(8,128)}), f32[64,8,128]{2,1,0:T(8,128)S(1)}, u32[]{:S(2)}, u32[]{:S(2)}) %all-to-all-start.3) | async-done | bytes 262176 | tf_op jit(solution)/shard_map/all_to_all | solution.py:169
  111.1 0.7 slice_bitcast_fusion
  111.8 0.6 slice_bitcast_fusion.1
  (2 shorter events, 0.0 us)
Async XLA Ops:
  2.6 40.4 %all-to-all-start = ((bf16[32,128,128]{2,1,0:T(8,128)(2,1)}), bf16[32,128,128]{2,1,0:T(8,128)(2,1)S(1)}, u32[]{:S(2)}, u32[]{:S(2)}) async-start(bf16[32,128,128]{2,1,0:T(8,128)(2,1)} %broadcast_in_dim.11), calls=%async_computation | async-start | bytes 2097152 | tf_op jit(solution)/shard_map/all_to_all | solution.py:133
  16.1 0.7 copy-start.3
  17.3 0.7 copy-start.2
  43.0 1.0 copy-start
  90.7 7.0 %copy-start.1 = (f32[16,128]{1,0:T(8,128)S(1)}, f32[16,128]{1,0:T(8,128)}, u32[]{:S(2)}) copy-start(f32[16,128]{1,0:T(8,128)} %get-tuple-element.5) | copy-start | bytes 24580
  90.7 20.4 %all-to-all-start.3 = ((f32[64,8,128]{2,1,0:T(8,128)}), f32[64,8,128]{2,1,0:T(8,128)S(1)}, u32[]{:S(2)}, u32[]{:S(2)}) async-start(f32[64,8,128]{2,1,0:T(8,128)} %broadcast_in_dim.27), calls=%async_computation.3 | async-start | bytes 524288 | tf_op jit(solution)/shard_map/all_to_all | solution.py:169

commit v2 on v1

v2 whole, which is shorter than its diff:
```python
import functools
import math

import jax
import jax.numpy as jnp
from jax import lax
from jax.experimental import pallas as pl
from jax.experimental.pallas import tpu as pltpu
from jax.sharding import Mesh
from jax.sharding import PartitionSpec as P

BLK = 64
LANES = 128
COUNT = 16
STEP = 8
MASKED = -1e30
EPS = 1e-06
HIGHEST = lax.Precision.HIGHEST

CTX = ("y", "zl")
SCATTER = ("x", "y")
REST = ("zh", "zl", "c")


def dot(a, b, dims):
    return lax.dot_general(
        a, b, (dims, ((), ())), precision=HIGHEST, preferred_element_type=jnp.float32
    )


def scores(k, q):
    return lax.dot_general(k, q, (((1,), (1,)), ((), ())), preferred_element_type=jnp.float32)


def lane_part(rows, toks):
    tok = lax.rem(lax.broadcasted_iota(jnp.int32, (1, rows), 1), toks)
    return tok // BLK, lax.rem(tok, BLK)


def lane_block(scal, part, own):
    block = jnp.zeros_like(part)
    for i in range(own):
        block = jnp.where(part == i, scal[1 + i], block)
    return block


def tile_sum(s, new, scale):
    e = jnp.exp2((s - new) * scale)
    return jnp.sum(e.reshape(s.shape[0] // 8, 8, s.shape[1]), axis=0)


def first_kernel(group, q_ref, k_ref, wq, high_ref, total_ref, pq_ref, xq_ref):
    rows, dim = q_ref.shape
    toks = rows // group
    own = toks // BLK
    scale = math.log2(math.e) / math.sqrt(dim)
    part, pos = lane_part(rows, toks)
    q = q_ref[...]
    s = scores(k_ref[...], q)
    tile = s[0:BLK]
    for i in range(1, own):
        tile = jnp.where(part == i, s[i * BLK : (i + 1) * BLK], tile)
    tile = jnp.where(lax.broadcasted_iota(jnp.int32, (BLK, rows), 0) <= pos, tile, MASKED)
    high = jnp.max(tile, axis=0, keepdims=True)
    high_ref[...] = high
    total_ref[...] = tile_sum(tile, high, scale)
    pq = jnp.sum(q.astype(jnp.float32).reshape(group * own, BLK, dim), axis=1) * (1.0 / BLK)
    pq = jnp.concatenate([pq, jnp.zeros((COUNT - group * own, dim), jnp.float32)], axis=0)
    pq_ref[...] = pq
    xq_ref[...] = dot(pq, wq[...], ((1,), (0,)))


def kernel(
    group, blocks, scal, order, q_ref, k_ref, ordv, high_ref, total_ref, pq_ref, xq_ref, wk,
    t_ref, g_ref, m_ref, pk_ref, s0, s1,
):
    rows, dim = q_ref.shape
    toks = rows // group
    own = toks // BLK
    length = scal[0]
    scale = math.log2(math.e) / math.sqrt(dim)
    width = STEP * BLK
    part, pos = lane_part(rows, toks)
    block = lane_block(scal, part, own)
    q = q_ref[...]
    diag = high_ref[...]
    m_ref[blocks:, :] = jnp.full((m_ref.shape[0] - blocks, rows), MASKED, jnp.float32)

    def fill(c, s_ref):
        k = k_ref[pl.ds(pl.multiple_of(c * width, width), width), :]
        s = scores(k, q)
        s_ref[...] = s
        tops = []
        for j in range(STEP):
            top = jnp.max(s[j * BLK : (j + 1) * BLK], axis=0, keepdims=True)
            kb = order[c * STEP + j]
            tops.append(jnp.where(block > kb, top, jnp.where(block == kb, diag, MASKED)))
        top = jnp.concatenate(tops, axis=0)
        at = pl.ds(pl.multiple_of(c * STEP, STEP), STEP)
        m_ref[at, :] = top
        kf = k.astype(jnp.float32).reshape(STEP, BLK, dim)
        pk_ref[at, 0:dim] = jnp.max(kf, axis=1)
        pk_ref[at, dim : 2 * dim] = jnp.min(kf, axis=1)
        pk_ref[at, 2 * dim : 3 * dim] = jnp.sum(kf, axis=1) * (1.0 / BLK)
        return jnp.max(top, axis=0, keepdims=True)

    def drain(c, s_ref, top, high, total):
        new = jnp.maximum(high, top)
        total = total * jnp.exp2((high - new) * scale)
        for j in range(STEP):
            fresh = tile_sum(s_ref[j * BLK : (j + 1) * BLK, :], new, scale)
            total = total + jnp.where(block > order[c * STEP + j], fresh, 0.0)
        return new, total

    def pair(p, carry):
        high, total, top = carry
        c = 2 * p
        high, total = drain(c, s0, top, high, total)
        top = fill(c + 1, s1)
        high, total = drain(c + 1, s1, top, high, total)
        top = fill(c + 2, s0)
        return high, total, top

    chunks = blocks // STEP
    top = fill(0, s0)
    high, total, top = lax.fori_loop(0, chunks // 2 - 1, pair, (diag, total_ref[...], top))
    high, total = drain(chunks - 2, s0, top, high, total)
    top = fill(chunks - 1, s1)
    high, total = drain(chunks - 1, s1, top, high, total)

    log_total = jnp.log2(jnp.sum(total, axis=0, keepdims=True))
    depth = jnp.where(pos + block * BLK < length, (m_ref[...] - high) * scale - log_total, MASKED)
    depth = jnp.max(jnp.transpose(depth).reshape(group * own, BLK, LANES), axis=1)[:, :blocks]
    pad = COUNT - group * own
    depth = jnp.concatenate([depth, jnp.full((pad, blocks), MASKED, jnp.float32)], axis=0)
    pooled = jnp.exp2(depth)
    row = lax.broadcasted_iota(jnp.int32, (COUNT, 1), 0)
    qblock = lane_block(scal, lax.rem(row, own), own)
    good = (qblock * BLK < length) & (row < group * own)
    totals = jnp.sum(pooled, axis=1, keepdims=True)
    target = jnp.where(good, pooled / jnp.where(good, totals, 1.0), 0.0)
    t_ref[...] = target

    pq = pq_ref[...]
    xq = xq_ref[...]
    pk = pk_ref[...]
    xk = dot(pk, wk[...], ((1,), (0,)))
    rq = lax.rsqrt(jnp.mean(xq * xq, axis=1, keepdims=True) + EPS)
    rk = lax.rsqrt(jnp.mean(xk * xk, axis=1, keepdims=True) + EPS)
    uq = xq * rq
    uk = xk * rk
    gate_scale = 1.0 / math.sqrt(xq.shape[1])
    logits = dot(uq, uk, ((1,), (1,))) * gate_scale
    kblock = ordv[...]
    allowed = (kblock <= qblock) & (kblock * BLK < length)
    weights = jnp.where(allowed, jnp.exp(logits), 0.0)
    soft = weights / jnp.sum(weights, axis=1, keepdims=True)
    dl = (soft * jnp.sum(target, axis=1, keepdims=True) - target) * gate_scale
    duq = dot(dl, uk, ((1,), (0,)))
    duk = dot(dl, uq, ((0,), (0,)))
    dxq = rq * (duq - uq * jnp.mean(duq * uq, axis=1, keepdims=True))
    dxk = rk * (duk - uk * jnp.mean(duk * uk, axis=1, keepdims=True))
    g_ref[0:dim, :] = dot(pq, dxq, ((0,), (0,)))
    g_ref[dim : 4 * dim, :] = dot(pk, dxk, ((0,), (0,)))


def body(queries, key_rows, block_order, conv_len, gate_wq, gate_wk):
    toks = queries.shape[1]
    group = queries.shape[2]
    dim = queries.shape[3]
    own = toks // BLK
    rows = group * toks
    blocks = block_order.shape[0]
    width = gate_wq.shape[1]
    ctx = lax.axis_size(CTX)
    key_own = key_rows[0, :, 0, :]
    keys = lax.all_to_all(
        jnp.broadcast_to(key_own[None], (ctx, toks, dim)), CTX, 0, 0, tiled=True
    ).reshape(ctx * toks, dim)
    length = lax.dynamic_index_in_dim(conv_len, lax.axis_index(("zh", "c")))
    mine = lax.dynamic_slice_in_dim(block_order, lax.axis_index(CTX) * own, own)
    scal = jnp.concatenate([length, mine])
    q = jnp.transpose(queries[0], (1, 0, 2)).reshape(rows, dim)
    smem = pl.BlockSpec(memory_space=pltpu.SMEM)
    vmem = pl.BlockSpec(memory_space=pltpu.VMEM)

    def f32(*shape):
        return jax.ShapeDtypeStruct(shape, jnp.float32)

    first = pl.pallas_call(
        functools.partial(first_kernel, group),
        out_shape=(f32(1, rows), f32(8, rows), f32(COUNT, dim), f32(COUNT, width)),
        in_specs=[vmem] * 3,
        out_specs=(vmem,) * 4,
        name="own_block",
    )(q, key_own, gate_wq)
    target, grads = pl.pallas_call(
        functools.partial(kernel, group, blocks),
        out_shape=(f32(COUNT, blocks), f32(4 * dim, width)),
        in_specs=[smem, smem] + [vmem] * 8,
        out_specs=(vmem, vmem),
        scratch_shapes=[
            pltpu.VMEM((LANES, rows), jnp.float32),
            pltpu.VMEM((blocks, 3 * dim), jnp.float32),
            pltpu.VMEM((STEP * BLK, rows), jnp.float32),
            pltpu.VMEM((STEP * BLK, rows), jnp.float32),
        ],
        name="teacher_gate",
    )(scal, block_order, q, keys, block_order[None], *first, gate_wk)

    parts = lax.axis_size(SCATTER)
    rest = lax.axis_size(REST)
    piece = 4 * dim // parts
    share = lax.all_to_all(grads.reshape(parts, piece, width), SCATTER, 0, 0, tiled=True)
    share = jnp.sum(share, axis=0)
    share = lax.all_to_all(
        jnp.broadcast_to(share[None], (rest, piece, width)), REST, 0, 0, tiled=True
    )
    share = jnp.sum(share, axis=0)
    grads = lax.all_to_all(
        jnp.broadcast_to(share[None], (parts, piece, width)), SCATTER, 0, 0, tiled=True
    ).reshape(4 * dim, width)
    target = target[: group * own].reshape(1, group, own, blocks)
    return target, grads[:dim], grads[dim:]


def solution(mesh):
    fine = Mesh(mesh.devices.reshape(8, 4, 4, 2, 2), ("y", "zl", "x", "zh", "c"))
    rows = P(("zh", "c"), CTX, "x", None)
    return jax.shard_map(
        body,
        mesh=fine,
        in_specs=(rows, rows, P(), P(), P(), P()),
        out_specs=(P(("zh", "c"), "x", CTX, None), P(), P()),
        check_vma=False,
    )
```

time: 113 us -> 107 us (0.947); the launches traced: 112 us -> 105 us
  waiting for transfers between devices: 36 us -> 31.8 us
  starting transfers between devices: 20.5 us -> 17.6 us
    all_to_all x1, blocking collectives: 23.3 us -> 16.5 us  [body(): lax.all_to_all(grads.reshape(parts, piece, width), SCATTER, 0, 0, tiled=T...]
    all_to_all x1, blocking collectives: 14.1 us -> 20.5 us  [body(): lax.all_to_all(jnp.broadcast_to(share[None], (rest, piece, width)), REST,...]
    all_to_all x2, waiting for transfers between devices: 36 us -> 31.8 us  [the longest x1 22 us: body(): lax.all_to_all(jnp.broadcast_to(key_own[None], (ctx, toks, dim)), CTX, 0,...]
    all_to_all x2, starting transfers between devices: 20.5 us -> 17.6 us  [the longest x1 13.5 us: body(): lax.all_to_all(jnp.broadcast_to(key_own[None], (ctx, toks, dim)), CTX, 0,...]
    broadcast_in_dim x4 -> x3, local copies, waits for them, and re-layouts: 3.22 us -> 2.68 us  [the longest x1 1.96 us: body(): jnp.broadcast_to(key_own[None], (ctx, toks, dim))]
    pallas_call x1 -> x2, Pallas kernels: 8.57 us -> 8.75 us  [the longest x1 6.94 us: body(): pl.pallas_call(functools.partial(kernel, group, blocks), out_shape=(f32(C...]
  transfers between devices with their start and end apart: 2 -> 2, of which waited for: 2 -> 2; matrix products, arithmetic and copies ran while one was open for 3% -> 2% of each run, Pallas kernels for 0% -> 2%
where the time goes in v2:
time: 107 us; the launch traced here: 105 us
  blocking collectives  37 us (35%)
  waiting for transfers between devices  31.8 us (30%)
  starting transfers between devices  17.6 us (16%)
  Pallas kernels  8.75 us (8%)
  local copies, waits for them, and re-layouts  7.51 us (7%)
  other arithmetic  1.25 us (1%)
    all_to_all x1, waiting for transfers between devices, body(): lax.all_to_all(jnp.broadcast_to(key_own[None], (ctx, toks, dim)), CTX, 0,...  22 us
    all_to_all x1, blocking collectives, body(): lax.all_to_all(jnp.broadcast_to(share[None], (rest, piece, width)), REST,...  20.5 us
    all_to_all x1, blocking collectives, body(): lax.all_to_all(grads.reshape(parts, piece, width), SCATTER, 0, 0, tiled=T...  16.5 us
    all_to_all x1, starting transfers between devices, body(): lax.all_to_all(jnp.broadcast_to(key_own[None], (ctx, toks, dim)), CTX, 0,...  13.5 us
    all_to_all x1, waiting for transfers between devices, body(): lax.all_to_all(jnp.broadcast_to(share[None], (parts, piece, width)), SCAT...  9.83 us
    pallas_call x1, Pallas kernels, body(): pl.pallas_call(functools.partial(kernel, group, blocks), out_shape=(f32(C...  6.94 us
    all_to_all x1, starting transfers between devices, body(): lax.all_to_all(jnp.broadcast_to(share[None], (parts, piece, width)), SCAT...  4.16 us
    unnamed x8, local copies, waits for them, and re-layouts  2.27 us
  transfers between devices with their start and end apart: 2, of which 2 were waited for; matrix products, arithmetic and copies ran while one was open for 2% of the time, Pallas kernels for 2%

profile of v2, /device:TPU:1, one launch (start us, length us, event | category | flops | bytes accessed | tf_op | source)
XLA Modules:
  0.0 104.7 jit_solution(13578522649055657229)
XLA Ops:
  0.6 2.0 %broadcast_in_dim.11 = bf16[32,128,128]{2,1,0:T(8,128)(2,1)} broadcast(bf16[128,128]{1,0:T(8,128)(2,1)} %bitcast.17), dimensions={1,2} | broadcast | bytes 1081344 | tf_op jit(solution)/shard_map/broadcast_in_dim | solution.py:178
  2.6 13.5 %all-to-all-start = ((bf16[32,128,128]{2,1,0:T(8,128)(2,1)}), bf16[32,128,128]{2,1,0:T(8,128)(2,1)S(1)}, u32[]{:S(2)}, u32[]{:S(2)}) async-start(bf16[32,128,128]{2,1,0:T(8,128)(2,1)} %broadcast_in_dim.11), calls=%async_computation | async-start | bytes 2097152 | tf_op jit(solution)/shard_map/all_to_all | solution.py:177
  16.1 0.0 copy-start.2
  16.1 0.6 copy-done.2
  16.7 0.1 dynamic_slice.8
  16.8 0.0 copy-start.3
  16.8 0.7 copy-done.3
  17.4 0.6 dynamic_slice.7
  18.0 1.8 %own_block.1 = (f32[1,640]{1,0:T(1,128)}, f32[8,640]{1,0:T(8,128)}, f32[16,128]{1,0:T(8,128)}, f32[16,128]{1,0:T(8,128)}) custom-call(bf16[640,128]{1,0:T(8,128)(2,1)} %bitcast.13, bf16[128,128]{1,0:T(8,128)(2,1)} %bitcast.18, f32[128,128]{1,0:T(8,128)} %wq.1), custom_call_target="tpu_custom_call" | custom-call | tf_op jit(solution)/shard_map/own_block/pallas_call | solution.py:190
  19.8 1.2 %pad_add_fusion.scal = s32[3]{0:T(128)} fusion(s32[2]{0:T(128)S(1)} %dynamic_slice.8, s32[1]{0:T(128)} %dynamic_slice.7), kind=kLoop, calls=%fused_computation | loop fusion | flops 3 | bytes 24 | tf_op jit(solution)/shard_map/concatenate | solution.py:182
  21.0 22.0 %all-to-all-done = bf16[32,128,128]{2,1,0:T(8,128)(2,1)S(1)} async-done(((bf16[32,128,128]{2,1,0:T(8,128)(2,1)}), bf16[32,128,128]{2,1,0:T(8,128)(2,1)S(1)}, u32[]{:S(2)}, u32[]{:S(2)}) %all-to-all-start) | async-done | bytes 1048608 | tf_op jit(solution)/shard_map/all_to_all | solution.py:177
  43.0 0.0 copy-start
  43.0 1.0 copy-done
  44.0 6.9 %teacher_gate.1 = (f32[16,64]{1,0:T(8,128)}, f32[512,128]{1,0:T(8,128)}) custom-call(s32[3]{0:T(128)} %pad_add_fusion.scal, s32[64]{0:T(128)} %order.1, bf16[640,128]{1,0:T(8,128)(2,1)} %bitcast.14, bf16[4096,128]{1,0:T(8,128)(2,1)} %bitcast.12, s32[1,64]{1,0:T(1,128)} %bitcast.21, f32[1,640]{1,0:T(1,128)} %get-tuple-element.9.high_ref, ...), custom_call_target="tpu_custom_call" | custom-call | tf_op jit(solution)/shard_map/teacher_gate/pallas_call | solution.py:197
  50.9 16.5 %all_to_all.20 = f32[32,16,128]{2,1,0:T(8,128)S(1)} all-to-all(f32[32,16,128]{2,1,0:T(8,128)} %bitcast.15), channel_id=1, replica_groups=mesh['y'=8,'zl'=4,'x'=4,'zh'=2,'c'=2] {'x','y'}, dimensions={0} | all-to-all | bytes 524288 | tf_op jit(solution)/shard_map/all_to_all | solution.py:214
  67.5 20.5 %all_to_all.21 = f32[16,16,128]{2,1,0:T(8,128)S(1)} all-to-all(f32[16,16,128]{2,1,0:T(8,128)S(1)} %broadcast_in_dim.25), channel_id=1, replica_groups=mesh['y'=8,'zl'=4,'x'=4,'zh'=2,'c'=2] {'zh','zl','c'}, dimensions={0} | all-to-all | bytes 262144 | tf_op jit(solution)/shard_map/all_to_all | solution.py:216
  88.0 0.7 broadcast_in_dim.26
  88.7 0.0 copy-start.1
  88.7 4.2 %all-to-all-start.3 = ((f32[32,16,128]{2,1,0:T(8,128)}), f32[32,16,128]{2,1,0:T(8,128)S(1)}, u32[]{:S(2)}, u32[]{:S(2)}) async-start(f32[32,16,128]{2,1,0:T(8,128)} %broadcast_in_dim.26), calls=%async_computation.3 | async-start | bytes 524288 | tf_op jit(solution)/shard_map/all_to_all | solution.py:220
  92.9 0.0 copy-done.1
  92.9 0.6 reshape.26
  93.5 9.8 %all-to-all-done.3 = f32[32,16,128]{2,1,0:T(8,128)S(1)} async-done(((f32[32,16,128]{2,1,0:T(8,128)}), f32[32,16,128]{2,1,0:T(8,128)S(1)}, u32[]{:S(2)}, u32[]{:S(2)}) %all-to-all-start.3) | async-done | bytes 262176 | tf_op jit(solution)/shard_map/all_to_all | solution.py:220
  103.3 0.6 slice.20
  104.0 0.7 slice.21
  (3 shorter events, 0.1 us)
Async XLA Ops:
  2.6 40.4 %all-to-all-start = ((bf16[32,128,128]{2,1,0:T(8,128)(2,1)}), bf16[32,128,128]{2,1,0:T(8,128)(2,1)S(1)}, u32[]{:S(2)}, u32[]{:S(2)}) async-start(bf16[32,128,128]{2,1,0:T(8,128)(2,1)} %broadcast_in_dim.11), calls=%async_computation | async-start | bytes 2097152 | tf_op jit(solution)/shard_map/all_to_all | solution.py:177
  16.1 0.7 copy-start.2
  16.8 0.7 copy-start.3
  43.0 1.0 copy-start
  88.7 4.2 %copy-start.1 = (f32[16,64]{1,0:T(8,128)S(1)}, f32[16,64]{1,0:T(8,128)}, u32[]{:S(2)}) copy-start(f32[16,64]{1,0:T(8,128)} %get-tuple-element.13) | copy-start | bytes 12292
  88.7 14.6 %all-to-all-start.3 = ((f32[32,16,128]{2,1,0:T(8,128)}), f32[32,16,128]{2,1,0:T(8,128)S(1)}, u32[]{:S(2)}, u32[]{:S(2)}) async-start(f32[32,16,128]{2,1,0:T(8,128)} %broadcast_in_dim.26), calls=%async_computation.3 | async-start | bytes 524288 | tf_op jit(solution)/shard_map/all_to_all | solution.py:220

commit v3 on v2

--- a/solution.py
+++ b/solution.py
@@ -45,8 +45,43 @@
 
 
 def tile_sum(s, new, scale):
-    e = jnp.exp2((s - new) * scale)
-    return jnp.sum(e.reshape(s.shape[0] // 8, 8, s.shape[1]), axis=0)
+    e = jnp.exp2((s.reshape(s.shape[0] // 8, 8, s.shape[1]) - new) * scale)
+    return jnp.sum(e, axis=0)
+
+
+def spread(x, op):
+    for shift in (4, 2, 1):
+        x = op(x, pltpu.roll(x, shift, 0))
+    return x
+
+
+def fold8(parts, op):
+    sub = lax.broadcasted_iota(jnp.int32, parts[0].shape, 0)
+    low = sub < 4
+    t = []
+    for i in range(4):
+        a, b = parts[i], parts[i + 4]
+        t.append(op(jnp.where(low, a, b), pltpu.roll(jnp.where(low, b, a), 4, 0)))
+    for shift in (2, 1):
+        half = len(t) // 2
+        low = lax.rem(sub, 2 * shift) < shift
+        t = [
+            jnp.where(
+                low,
+                op(t[i], pltpu.roll(t[i], 8 - shift, 0)),
+                op(t[i + half], pltpu.roll(t[i + half], shift, 0)),
+            )
+            for i in range(half)
+        ]
+    return t[0]
+
+
+def fold_keys(k, reduce, op):
+    parts = [
+        reduce(k[j * BLK : (j + 1) * BLK].reshape(BLK // 8, 8, k.shape[1]), axis=0)
+        for j in range(STEP)
+    ]
+    return fold8(parts, op)
 
 
 def first_kernel(group, q_ref, k_ref, wq, high_ref, total_ref, pq_ref, xq_ref):
@@ -70,66 +105,96 @@
     xq_ref[...] = dot(pq, wq[...], ((1,), (0,)))
 
 
-def kernel(
-    group, blocks, scal, order, q_ref, k_ref, ordv, high_ref, total_ref, pq_ref, xq_ref, wk,
-    t_ref, g_ref, m_ref, pk_ref, s0, s1,
-):
-    rows, dim = q_ref.shape
-    toks = rows // group
-    own = toks // BLK
-    length = scal[0]
+def scan_keys(own, scal, order, odd, q, k_ref, ordc, diag, high, total, m_ref, pk_ref, s0, s1):
+    rows, dim = q.shape
+    toks = own * BLK
     scale = math.log2(math.e) / math.sqrt(dim)
     width = STEP * BLK
-    part, pos = lane_part(rows, toks)
-    block = lane_block(scal, part, own)
-    q = q_ref[...]
-    diag = high_ref[...]
-    m_ref[blocks:, :] = jnp.full((m_ref.shape[0] - blocks, rows), MASKED, jnp.float32)
+    part, _ = lane_part(rows, toks)
+    block8 = jnp.broadcast_to(lane_block(scal, part, own), (8, rows))
+    diag = jnp.broadcast_to(diag, (8, rows))
+    col = lax.broadcasted_iota(jnp.int32, (STEP, width), 1) // BLK
+    mean = jnp.where(col == lax.broadcasted_iota(jnp.int32, (STEP, width), 0), 1.0 / BLK, 0.0)
+    mean = mean.astype(k_ref.dtype)
 
     def fill(c, s_ref):
         k = k_ref[pl.ds(pl.multiple_of(c * width, width), width), :]
         s = scores(k, q)
         s_ref[...] = s
-        tops = []
-        for j in range(STEP):
-            top = jnp.max(s[j * BLK : (j + 1) * BLK], axis=0, keepdims=True)
-            kb = order[c * STEP + j]
-            tops.append(jnp.where(block > kb, top, jnp.where(block == kb, diag, MASKED)))
-        top = jnp.concatenate(tops, axis=0)
-        at = pl.ds(pl.multiple_of(c * STEP, STEP), STEP)
+        tops = [
+            jnp.max(s[j * BLK : (j + 1) * BLK].reshape(BLK // 8, 8, rows), axis=0)
+            for j in range(STEP)
+        ]
+        top = fold8(tops, jnp.maximum)
+        at = pl.ds(pl.multiple_of((2 * c + odd) * STEP, STEP), STEP)
+        kb = jnp.tile(ordc[at, :], (1, rows // LANES))
+        top = jnp.where(block8 > kb, top, jnp.where(block8 == kb, diag, MASKED))
         m_ref[at, :] = top
-        kf = k.astype(jnp.float32).reshape(STEP, BLK, dim)
-        pk_ref[at, 0:dim] = jnp.max(kf, axis=1)
-        pk_ref[at, dim : 2 * dim] = jnp.min(kf, axis=1)
-        pk_ref[at, 2 * dim : 3 * dim] = jnp.sum(kf, axis=1) * (1.0 / BLK)
-        return jnp.max(top, axis=0, keepdims=True)
+        kf = k.astype(jnp.float32)
+        pk_ref[at, 0:dim] = fold_keys(kf, jnp.max, jnp.maximum)
+        pk_ref[at, dim : 2 * dim] = fold_keys(kf, jnp.min, jnp.minimum)
+        pk_ref[at, 2 * dim : 3 * dim] = lax.dot_general(
+            mean, k, (((1,), (0,)), ((), ())), preferred_element_type=jnp.float32
+        )
+        return spread(top, jnp.maximum)
 
     def drain(c, s_ref, top, high, total):
         new = jnp.maximum(high, top)
         total = total * jnp.exp2((high - new) * scale)
         for j in range(STEP):
             fresh = tile_sum(s_ref[j * BLK : (j + 1) * BLK, :], new, scale)
-            total = total + jnp.where(block > order[c * STEP + j], fresh, 0.0)
+            total = total + jnp.where(block8 > order[(2 * c + odd) * STEP + j], fresh, 0.0)
         return new, total
 
-    def pair(p, carry):
-        high, total, top = carry
-        c = 2 * p
-        high, total = drain(c, s0, top, high, total)
-        top = fill(c + 1, s1)
-        high, total = drain(c + 1, s1, top, high, total)
-        top = fill(c + 2, s0)
-        return high, total, top
-
-    chunks = blocks // STEP
+    chunks = k_ref.shape[0] // width
+    bufs = (s0, s1)
     top = fill(0, s0)
-    high, total, top = lax.fori_loop(0, chunks // 2 - 1, pair, (diag, total_ref[...], top))
-    high, total = drain(chunks - 2, s0, top, high, total)
-    top = fill(chunks - 1, s1)
-    high, total = drain(chunks - 1, s1, top, high, total)
+    for c in range(chunks):
+        ahead = fill(c + 1, bufs[(c + 1) % 2]) if c + 1 < chunks else None
+        high, total = drain(c, bufs[c % 2], top, high, total)
+        top = ahead
+    return high, total
+
+
+def half_kernel(
+    own, scal, order, q_ref, k_ref, ordc, high_ref, total_ref,
+    high_out, total_out, m_ref, pk_ref, s0, s1,
+):
+    diag = high_ref[...]
+    high = jnp.broadcast_to(diag, high_out.shape)
+    m_ref[...] = jnp.full(m_ref.shape, MASKED, jnp.float32)
+    pk_ref[...] = jnp.zeros(pk_ref.shape, jnp.float32)
+    high, total = scan_keys(
+        own, scal, order, scal[1 + own], q_ref[...], k_ref, ordc, diag, high, total_ref[...],
+        m_ref, pk_ref, s0, s1,
+    )
+    high_out[...] = high
+    total_out[...] = total
+
+
+def kernel(
+    own, scal, order, q_ref, k_ref, ordv, ordc, diag_ref, high_ref, total_ref, m_in, pk_in,
+    pq_ref, xq_ref, wk, t_ref, g_ref, m_ref, pk_ref, s0, s1,
+):
+    rows, dim = q_ref.shape
+    toks = own * BLK
+    group = rows // toks
+    blocks = order.shape[0]
+    length = scal[0]
+    odd = scal[1 + own]
+    scale = math.log2(math.e) / math.sqrt(dim)
+    part, pos = lane_part(rows, toks)
+    block = lane_block(scal, part, own)
+    m_ref[...] = jnp.full(m_ref.shape, MASKED, jnp.float32)
+    high, total = scan_keys(
+        own, scal, order, 1 - odd, q_ref[...], k_ref, ordc, diag_ref[...], high_ref[...],
+        total_ref[...], m_ref, pk_ref, s0, s1,
+    )
+    seen = lax.rem(lax.broadcasted_iota(jnp.int32, (blocks, 1), 0) // STEP, 2) == odd
+    m_ref[0:blocks, :] = jnp.where(seen, m_in[...], m_ref[0:blocks, :])
 
     log_total = jnp.log2(jnp.sum(total, axis=0, keepdims=True))
-    depth = jnp.where(pos + block * BLK < length, (m_ref[...] - high) * scale - log_total, MASKED)
+    depth = jnp.where(pos + block * BLK < length, (m_ref[...] - high[0:1]) * scale - log_total, MASKED)
     depth = jnp.max(jnp.transpose(depth).reshape(group * own, BLK, LANES), axis=1)[:, :blocks]
     pad = COUNT - group * own
     depth = jnp.concatenate([depth, jnp.full((pad, blocks), MASKED, jnp.float32)], axis=0)
@@ -143,7 +208,7 @@
 
     pq = pq_ref[...]
     xq = xq_ref[...]
-    pk = pk_ref[...]
+    pk = jnp.where(seen, pk_in[...], pk_ref[...])
     xk = dot(pk, wk[...], ((1,), (0,)))
     rq = lax.rsqrt(jnp.mean(xq * xq, axis=1, keepdims=True) + EPS)
     rk = lax.rsqrt(jnp.mean(xk * xk, axis=1, keepdims=True) + EPS)
@@ -172,15 +237,26 @@
     rows = group * toks
     blocks = block_order.shape[0]
     width = gate_wq.shape[1]
-    ctx = lax.axis_size(CTX)
     key_own = key_rows[0, :, 0, :]
-    keys = lax.all_to_all(
-        jnp.broadcast_to(key_own[None], (ctx, toks, dim)), CTX, 0, 0, tiled=True
-    ).reshape(ctx * toks, dim)
+    ny, nz = lax.axis_size("y"), lax.axis_size("zl")
+    odd = lax.rem(lax.axis_index("y"), 2)
+    peers = ny // 2 * nz
+    same = [[y * nz + z for y in range(h, ny, 2) for z in range(nz)] for h in range(2)]
+    near = lax.all_to_all(
+        jnp.broadcast_to(key_own[None], (peers, toks, dim)),
+        CTX, 0, 0, axis_index_groups=same, tiled=True,
+    ).reshape(peers * toks, dim)
+    pairs = []
+    for y in range(ny):
+        for c in range(2):
+            other = y + 1 if y % 2 == c else y - 1
+            pairs.append((2 * y + c, 2 * (other % ny) + c))
+    far = lax.ppermute(near, ("y", "c"), pairs)
     length = lax.dynamic_index_in_dim(conv_len, lax.axis_index(("zh", "c")))
     mine = lax.dynamic_slice_in_dim(block_order, lax.axis_index(CTX) * own, own)
-    scal = jnp.concatenate([length, mine])
+    scal = jnp.concatenate([length, mine, odd[None]])
     q = jnp.transpose(queries[0], (1, 0, 2)).reshape(rows, dim)
+    ordc = jnp.broadcast_to(block_order[:, None], (blocks, LANES))
     smem = pl.BlockSpec(memory_space=pltpu.SMEM)
     vmem = pl.BlockSpec(memory_space=pltpu.VMEM)
 
@@ -194,19 +270,32 @@
         out_specs=(vmem,) * 4,
         name="own_block",
     )(q, key_own, gate_wq)
+    high, total, pq, xq = first
+    buffers = [pltpu.VMEM((STEP * BLK, rows), jnp.float32)] * 2
+    after, total, m_half, pk_half = pl.pallas_call(
+        functools.partial(half_kernel, own),
+        out_shape=(f32(8, rows), f32(8, rows), f32(blocks, rows), f32(blocks, 3 * dim)),
+        in_specs=[smem, smem] + [vmem] * 5,
+        out_specs=(vmem,) * 4,
+        scratch_shapes=buffers,
+        name="teacher_near",
+    )(scal, block_order, q, pltpu.with_memory_space_constraint(near, pltpu.VMEM), ordc, high, total)
     target, grads = pl.pallas_call(
-        functools.partial(kernel, group, blocks),
+        functools.partial(kernel, own),
         out_shape=(f32(COUNT, blocks), f32(4 * dim, width)),
-        in_specs=[smem, smem] + [vmem] * 8,
+        in_specs=[smem, smem] + [vmem] * 12,
         out_specs=(vmem, vmem),
         scratch_shapes=[
             pltpu.VMEM((LANES, rows), jnp.float32),
             pltpu.VMEM((blocks, 3 * dim), jnp.float32),
-            pltpu.VMEM((STEP * BLK, rows), jnp.float32),
-            pltpu.VMEM((STEP * BLK, rows), jnp.float32),
+            *buffers,
         ],
         name="teacher_gate",
-    )(scal, block_order, q, keys, block_order[None], *first, gate_wk)
+    )(
+        scal, block_order, q, pltpu.with_memory_space_constraint(far, pltpu.VMEM),
+        block_order[None], ordc, high, after, total, m_half, pk_half,
+        pq, xq, gate_wk,
+    )
 
     parts = lax.axis_size(SCATTER)
     rest = lax.axis_size(REST)

time: 107 us -> 104 us (0.972)
  blocking collectives: 37 us -> 67.5 us
  waiting for transfers between devices: 31.8 us -> 10.1 us
  starting transfers between devices: 17.6 us -> 6.27 us
  local copies, waits for them, and re-layouts: 7.51 us -> 6.08 us
  Pallas kernels: 8.75 us -> 10 us
    all_to_all x0 -> x1, blocking collectives: none -> 29.9 us  [body(): lax.all_to_all(jnp.broadcast_to(key_own[None], (peers, toks, dim)), CTX,...]
    all_to_all x1 -> x0, waiting for transfers between devices: 22 us -> none  [body(): lax.all_to_all(jnp.broadcast_to(key_own[None], (ctx, toks, dim)), CTX, 0,...]
    all_to_all x1 -> x0, starting transfers between devices: 13.5 us -> none  [body(): lax.all_to_all(jnp.broadcast_to(key_own[None], (ctx, toks, dim)), CTX, 0,...]
    ppermute x0 -> x1, starting transfers between devices: none -> 1.91 us  [body(): far = lax.ppermute(near, ('y', 'c'), pairs)]
    pallas_call x1 -> x2, Pallas kernels: 6.94 us -> 8.24 us  [the longest x1 4.9 us: body(): pl.pallas_call(functools.partial(kernel, own), out_shape=(f32(COUNT, bloc...]
    all_to_all x1, blocking collectives: 16.5 us -> 17.7 us  [body(): lax.all_to_all(grads.reshape(parts, piece, width), SCATTER, 0, 0, tiled=T...]
    unnamed x8 -> x6, local copies, waits for them, and re-layouts: 2.27 us -> 1.23 us
  transfers between devices with their start and end apart: 2 -> 2, of which waited for: 2 -> 2; matrix products, arithmetic and copies ran while one was open for 2% -> 3% of each run, Pallas kernels for 2% -> 5%
where the time goes in v3:
time: 104 us; the launch traced here: 102 us
  blocking collectives  67.5 us (65%)
  waiting for transfers between devices  10.1 us (10%)
  Pallas kernels  10 us (10%)
  starting transfers between devices  6.27 us (6%)
  local copies, waits for them, and re-layouts  6.08 us (6%)
  other arithmetic  1.28 us (1%)
    all_to_all x1, blocking collectives, body(): lax.all_to_all(jnp.broadcast_to(key_own[None], (peers, toks, dim)), CTX,...  29.9 us
    all_to_all x1, blocking collectives, body(): lax.all_to_all(jnp.broadcast_to(share[None], (rest, piece, width)), REST,...  19.9 us
    all_to_all x1, blocking collectives, body(): lax.all_to_all(grads.reshape(parts, piece, width), SCATTER, 0, 0, tiled=T...  17.7 us
    all_to_all x1, waiting for transfers between devices, body(): lax.all_to_all(jnp.broadcast_to(share[None], (parts, piece, width)), SCAT...  9.83 us
    pallas_call x1, Pallas kernels, body(): pl.pallas_call(functools.partial(kernel, own), out_shape=(f32(COUNT, bloc...  4.9 us
    all_to_all x1, starting transfers between devices, body(): lax.all_to_all(jnp.broadcast_to(share[None], (parts, piece, width)), SCAT...  4.36 us
    pallas_call x1, Pallas kernels, body(): pl.pallas_call(functools.partial(half_kernel, own), out_shape=(f32(8, row...  3.34 us
  transfers between devices with their start and end apart: 2, of which 2 were waited for; matrix products, arithmetic and copies ran while one was open for 3% of the time, Pallas kernels for 5%

profile of v3, /device:TPU:1, one launch (start us, length us, event | category | flops | bytes accessed | tf_op | source)
XLA Modules:
  0.0 102.0 jit_solution(8675530019817453605)
XLA Ops:
  0.6 0.9 broadcast_in_dim.16
  1.5 29.9 %all_to_all.20 = bf16[16,128,128]{2,1,0:T(8,128)(2,1)S(1)} all-to-all(bf16[16,128,128]{2,1,0:T(8,128)(2,1)S(1)} %broadcast_in_dim.16), channel_id=1, replica_groups={{0,16,32,48,128,144,160,176,256,272,288,304,384,400,416,432},{64,80,96,..., dimensions={0} | all-to-all | bytes 1048576 | tf_op jit(solution)/shard_map/all_to_all | solution.py:245
  31.4 1.9 %collective-permute-start = (bf16[2048,128]{1,0:T(8,128)(2,1)S(1)}, bf16[2048,128]{1,0:T(8,128)(2,1)S(1)}, u32[]{:S(2)}, u32[]{:S(2)}) collective-permute-start(bf16[2048,128]{1,0:T(8,128)(2,1)S(1)} %bitcast.13), channel_id=1, source_target_pairs={{0,64},{1,449},{64,0},{65,129},{128,192},{129,65},{192,128},{193,2... | collective-permute-start | bytes 1572872 | tf_op jit(solution)/shard_map/ppermute | solution.py:254
  33.3 0.0 copy-start
  33.3 0.6 copy-done
  34.0 0.0 copy-start.2
  34.0 0.1 dynamic_slice.8
  34.0 0.6 copy-done.2
  34.6 0.6 dynamic_slice.7
  35.2 1.8 %own_block.1 = (f32[1,640]{1,0:T(1,128)}, f32[8,640]{1,0:T(8,128)}, f32[16,128]{1,0:T(8,128)}, f32[16,128]{1,0:T(8,128)}) custom-call(bf16[640,128]{1,0:T(8,128)(2,1)} %bitcast.15, bf16[128,128]{1,0:T(8,128)(2,1)} %bitcast.21, f32[128,128]{1,0:T(8,128)} %wq.1), custom_call_target="tpu_custom_call" | custom-call | tf_op jit(solution)/shard_map/own_block/pallas_call | solution.py:266
  37.0 1.2 %pad_add_fusion.scal = s32[4]{0:T(128)} fusion(s32[1]{0:T(128)} %bitcast, s32[2]{0:T(128)S(1)} %dynamic_slice.8, s32[1]{0:T(128)} %dynamic_slice.7), kind=kLoop, calls=%fused_computation | loop fusion | flops 8 | bytes 32 | tf_op jit(solution)/shard_map/concatenate | solution.py:257
  38.2 0.7 broadcast_in_dim.35.ordc
  38.9 3.3 %teacher_near.1 = (f32[8,640]{1,0:T(8,128)}, f32[8,640]{1,0:T(8,128)}, f32[64,640]{1,0:T(8,128)}, f32[64,384]{1,0:T(8,128)}) custom-call(s32[4]{0:T(128)} %pad_add_fusion.scal, s32[64]{0:T(128)} %order.3, bf16[640,128]{1,0:T(8,128)(2,1)} %bitcast.16, bf16[2048,128]{1,0:T(8,128)(2,1)S(1)} %bitcast.14, s32[64,128]{1,0:T(8,128)} %broadcast_in_dim.35.ordc, ...), custom_call_target="tpu_custom_call" | custom-call | tf_op jit(solution)/shard_map/teacher_near/pallas_call | solution.py:275
  42.3 0.2 collective-permute-done.k_ref
  42.5 4.9 %teacher_gate.1 = (f32[16,64]{1,0:T(8,128)}, f32[512,128]{1,0:T(8,128)}) custom-call(s32[4]{0:T(128)} %pad_add_fusion.scal, s32[64]{0:T(128)} %order.3, bf16[640,128]{1,0:T(8,128)(2,1)} %bitcast.17, bf16[2048,128]{1,0:T(8,128)(2,1)S(1)} %collective-permute-done.k_ref, s32[1,64]{1,0:T(1,128)} %bitcast.23, s32[64,128]{1,0:T(8,128)} %broadcast_in_dim.35.ordc, ...), custom_call_target="tpu_custom_call" | custom-call | tf_op jit(solution)/shard_map/teacher_gate/pallas_call | solution.py:283
  47.4 17.7 %all_to_all.21 = f32[32,16,128]{2,1,0:T(8,128)S(1)} all-to-all(f32[32,16,128]{2,1,0:T(8,128)} %bitcast.18), channel_id=1, replica_groups=mesh['y'=8,'zl'=4,'x'=4,'zh'=2,'c'=2] {'x','y'}, dimensions={0} | all-to-all | bytes 524288 | tf_op jit(solution)/shard_map/all_to_all | solution.py:303
  65.2 19.9 %all_to_all.22 = f32[16,16,128]{2,1,0:T(8,128)S(1)} all-to-all(f32[16,16,128]{2,1,0:T(8,128)S(1)} %broadcast_in_dim.36), channel_id=1, replica_groups=mesh['y'=8,'zl'=4,'x'=4,'zh'=2,'c'=2] {'zh','zl','c'}, dimensions={0} | all-to-all | bytes 262144 | tf_op jit(solution)/shard_map/all_to_all | solution.py:305
  85.1 0.7 broadcast_in_dim.37
  85.8 0.0 copy-start.1
  85.8 4.4 %all-to-all-start.3 = ((f32[32,16,128]{2,1,0:T(8,128)}), f32[32,16,128]{2,1,0:T(8,128)S(1)}, u32[]{:S(2)}, u32[]{:S(2)}) async-start(f32[32,16,128]{2,1,0:T(8,128)} %broadcast_in_dim.37), calls=%async_computation.3 | async-start | bytes 524288 | tf_op jit(solution)/shard_map/all_to_all | solution.py:309
  90.2 0.0 copy-done.1
  90.2 0.6 reshape.27
  90.8 9.8 %all-to-all-done.3 = f32[32,16,128]{2,1,0:T(8,128)S(1)} async-done(((f32[32,16,128]{2,1,0:T(8,128)}), f32[32,16,128]{2,1,0:T(8,128)S(1)}, u32[]{:S(2)}, u32[]{:S(2)}) %all-to-all-start.3) | async-done | bytes 262176 | tf_op jit(solution)/shard_map/all_to_all | solution.py:309
  100.7 0.6 slice.20
  101.3 0.7 slice.21
  (3 shorter events, 0.1 us)
Async XLA Ops:
  31.4 11.1 %collective-permute-start = (bf16[2048,128]{1,0:T(8,128)(2,1)S(1)}, bf16[2048,128]{1,0:T(8,128)(2,1)S(1)}, u32[]{:S(2)}, u32[]{:S(2)}) collective-permute-start(bf16[2048,128]{1,0:T(8,128)(2,1)S(1)} %bitcast.13), channel_id=1, source_target_pairs={{0,64},{1,449},{64,0},{65,129},{128,192},{129,65},{192,128},{193,2... | collective-permute-start | bytes 1572872 | tf_op jit(solution)/shard_map/ppermute | solution.py:254
  33.3 0.7 copy-start
  34.0 0.7 copy-start.2
  85.8 4.4 %copy-start.1 = (f32[16,64]{1,0:T(8,128)S(1)}, f32[16,64]{1,0:T(8,128)}, u32[]{:S(2)}) copy-start(f32[16,64]{1,0:T(8,128)} %get-tuple-element.21) | copy-start | bytes 12292
  85.8 14.8 %all-to-all-start.3 = ((f32[32,16,128]{2,1,0:T(8,128)}), f32[32,16,128]{2,1,0:T(8,128)S(1)}, u32[]{:S(2)}, u32[]{:S(2)}) async-start(f32[32,16,128]{2,1,0:T(8,128)} %broadcast_in_dim.37), calls=%async_computation.3 | async-start | bytes 524288 | tf_op jit(solution)/shard_map/all_to_all | solution.py:309

commit v4 on v3

--- a/solution.py
+++ b/solution.py
@@ -105,7 +105,7 @@
     xq_ref[...] = dot(pq, wq[...], ((1,), (0,)))
 
 
-def scan_keys(own, scal, order, odd, q, k_ref, ordc, diag, high, total, m_ref, pk_ref, s0, s1):
+def scan_keys(own, scal, order, odd, q, k_ref, diag, high, total, m_ref, pk_ref, s0, s1):
     rows, dim = q.shape
     toks = own * BLK
     scale = math.log2(math.e) / math.sqrt(dim)
@@ -117,6 +117,8 @@
     mean = jnp.where(col == lax.broadcasted_iota(jnp.int32, (STEP, width), 0), 1.0 / BLK, 0.0)
     mean = mean.astype(k_ref.dtype)
 
+    sub = lax.broadcasted_iota(jnp.int32, (STEP, LANES), 0)
+
     def fill(c, s_ref):
         k = k_ref[pl.ds(pl.multiple_of(c * width, width), width), :]
         s = scores(k, q)
@@ -127,7 +129,10 @@
         ]
         top = fold8(tops, jnp.maximum)
         at = pl.ds(pl.multiple_of((2 * c + odd) * STEP, STEP), STEP)
-        kb = jnp.tile(ordc[at, :], (1, rows // LANES))
+        kb = jnp.zeros((STEP, LANES), jnp.int32)
+        for j in range(STEP):
+            kb = jnp.where(sub == j, order[(2 * c + odd) * STEP + j], kb)
+        kb = jnp.tile(kb, (1, rows // LANES))
         top = jnp.where(block8 > kb, top, jnp.where(block8 == kb, diag, MASKED))
         m_ref[at, :] = top
         kf = k.astype(jnp.float32)
@@ -157,7 +162,7 @@
 
 
 def half_kernel(
-    own, scal, order, q_ref, k_ref, ordc, high_ref, total_ref,
+    own, scal, order, q_ref, k_ref, high_ref, total_ref,
     high_out, total_out, m_ref, pk_ref, s0, s1,
 ):
     diag = high_ref[...]
@@ -165,7 +170,7 @@
     m_ref[...] = jnp.full(m_ref.shape, MASKED, jnp.float32)
     pk_ref[...] = jnp.zeros(pk_ref.shape, jnp.float32)
     high, total = scan_keys(
-        own, scal, order, scal[1 + own], q_ref[...], k_ref, ordc, diag, high, total_ref[...],
+        own, scal, order, scal[1 + own], q_ref[...], k_ref, diag, high, total_ref[...],
         m_ref, pk_ref, s0, s1,
     )
     high_out[...] = high
@@ -173,7 +178,7 @@
 
 
 def kernel(
-    own, scal, order, q_ref, k_ref, ordv, ordc, diag_ref, high_ref, total_ref, m_in, pk_in,
+    own, scal, order, q_ref, k_ref, ordv, diag_ref, high_ref, total_ref, m_in, pk_in,
     pq_ref, xq_ref, wk, t_ref, g_ref, m_ref, pk_ref, s0, s1,
 ):
     rows, dim = q_ref.shape
@@ -187,7 +192,7 @@
     block = lane_block(scal, part, own)
     m_ref[...] = jnp.full(m_ref.shape, MASKED, jnp.float32)
     high, total = scan_keys(
-        own, scal, order, 1 - odd, q_ref[...], k_ref, ordc, diag_ref[...], high_ref[...],
+        own, scal, order, 1 - odd, q_ref[...], k_ref, diag_ref[...], high_ref[...],
         total_ref[...], m_ref, pk_ref, s0, s1,
     )
     seen = lax.rem(lax.broadcasted_iota(jnp.int32, (blocks, 1), 0) // STEP, 2) == odd
@@ -204,7 +209,8 @@
     good = (qblock * BLK < length) & (row < group * own)
     totals = jnp.sum(pooled, axis=1, keepdims=True)
     target = jnp.where(good, pooled / jnp.where(good, totals, 1.0), 0.0)
-    t_ref[...] = target
+    for h in range(group):
+        t_ref[0, h] = target[own * h : own * (h + 1)]
 
     pq = pq_ref[...]
     xq = xq_ref[...]
@@ -229,6 +235,18 @@
     g_ref[dim : 4 * dim, :] = dot(pk, dxk, ((0,), (0,)))
 
 
+def split_kernel(g_ref, q_ref, k_ref, sem):
+    rows = q_ref.shape[0]
+    copies = [
+        pltpu.make_async_copy(g_ref.at[pl.ds(0, rows)], q_ref, sem.at[0]),
+        pltpu.make_async_copy(g_ref.at[pl.ds(rows, k_ref.shape[0])], k_ref, sem.at[1]),
+    ]
+    for copy in copies:
+        copy.start()
+    for copy in copies:
+        copy.wait()
+
+
 def body(queries, key_rows, block_order, conv_len, gate_wq, gate_wk):
     toks = queries.shape[1]
     group = queries.shape[2]
@@ -246,17 +264,10 @@
         jnp.broadcast_to(key_own[None], (peers, toks, dim)),
         CTX, 0, 0, axis_index_groups=same, tiled=True,
     ).reshape(peers * toks, dim)
-    pairs = []
-    for y in range(ny):
-        for c in range(2):
-            other = y + 1 if y % 2 == c else y - 1
-            pairs.append((2 * y + c, 2 * (other % ny) + c))
-    far = lax.ppermute(near, ("y", "c"), pairs)
     length = lax.dynamic_index_in_dim(conv_len, lax.axis_index(("zh", "c")))
     mine = lax.dynamic_slice_in_dim(block_order, lax.axis_index(CTX) * own, own)
     scal = jnp.concatenate([length, mine, odd[None]])
     q = jnp.transpose(queries[0], (1, 0, 2)).reshape(rows, dim)
-    ordc = jnp.broadcast_to(block_order[:, None], (blocks, LANES))
     smem = pl.BlockSpec(memory_space=pltpu.SMEM)
     vmem = pl.BlockSpec(memory_space=pltpu.VMEM)
 
@@ -270,20 +281,27 @@
         out_specs=(vmem,) * 4,
         name="own_block",
     )(q, key_own, gate_wq)
+    near, scal, first = lax.optimization_barrier((near, scal, first))
     high, total, pq, xq = first
+    pairs = []
+    for y in range(ny):
+        for c in range(2):
+            other = y + 1 if y % 2 == c else y - 1
+            pairs.append((2 * y + c, 2 * (other % ny) + c))
+    far = lax.ppermute(near, ("y", "c"), pairs)
     buffers = [pltpu.VMEM((STEP * BLK, rows), jnp.float32)] * 2
     after, total, m_half, pk_half = pl.pallas_call(
         functools.partial(half_kernel, own),
         out_shape=(f32(8, rows), f32(8, rows), f32(blocks, rows), f32(blocks, 3 * dim)),
-        in_specs=[smem, smem] + [vmem] * 5,
+        in_specs=[smem, smem] + [vmem] * 4,
         out_specs=(vmem,) * 4,
         scratch_shapes=buffers,
         name="teacher_near",
-    )(scal, block_order, q, pltpu.with_memory_space_constraint(near, pltpu.VMEM), ordc, high, total)
+    )(scal, block_order, q, pltpu.with_memory_space_constraint(near, pltpu.VMEM), high, total)
     target, grads = pl.pallas_call(
         functools.partial(kernel, own),
-        out_shape=(f32(COUNT, blocks), f32(4 * dim, width)),
-        in_specs=[smem, smem] + [vmem] * 12,
+        out_shape=(f32(1, group, own, blocks), f32(4 * dim, width)),
+        in_specs=[smem, smem] + [vmem] * 11,
         out_specs=(vmem, vmem),
         scratch_shapes=[
             pltpu.VMEM((LANES, rows), jnp.float32),
@@ -293,7 +311,7 @@
         name="teacher_gate",
     )(
         scal, block_order, q, pltpu.with_memory_space_constraint(far, pltpu.VMEM),
-        block_order[None], ordc, high, after, total, m_half, pk_half,
+        block_order[None], high, after, total, m_half, pk_half,
         pq, xq, gate_wk,
     )
 
@@ -309,8 +327,16 @@
     grads = lax.all_to_all(
         jnp.broadcast_to(share[None], (parts, piece, width)), SCATTER, 0, 0, tiled=True
     ).reshape(4 * dim, width)
-    target = target[: group * own].reshape(1, group, own, blocks)
-    return target, grads[:dim], grads[dim:]
+    anywhere = pl.BlockSpec(memory_space=pl.ANY)
+    grad_wq, grad_wk = pl.pallas_call(
+        split_kernel,
+        out_shape=(f32(dim, width), f32(3 * dim, width)),
+        in_specs=[vmem],
+        out_specs=(anywhere, anywhere),
+        scratch_shapes=[pltpu.SemaphoreType.DMA((2,))],
+        name="split_grads",
+    )(pltpu.with_memory_space_constraint(grads, pltpu.VMEM))
+    return target, grad_wq, grad_wk
 
 
 def solution(mesh):

time: 104 us -> 103 us (level)
  blocking collectives: 67.5 us -> 52.1 us
  starting transfers between devices: 6.27 us -> 15.1 us
  waiting for transfers between devices: 10.1 us -> 17.9 us
  local copies, waits for them, and re-layouts: 6.08 us -> 3.57 us
    all_to_all x1, blocking collectives: 29.9 us -> 14.4 us  [body(): lax.all_to_all(jnp.broadcast_to(share[None], (parts, piece, width)), SCAT...]
    all_to_all x1, starting transfers between devices: 4.36 us -> 13.2 us  [body(): lax.all_to_all(jnp.broadcast_to(key_own[None], (peers, toks, dim)), CTX,...]
    ppermute x1, waiting for transfers between devices: 0.24 us -> 5.89 us  [body(): far = lax.ppermute(near, ('y', 'c'), pairs)]
    all_to_all x1, waiting for transfers between devices: 9.83 us -> 12 us  [body(): lax.all_to_all(jnp.broadcast_to(key_own[None], (peers, toks, dim)), CTX,...]
    slice x2 -> x0, local copies, waits for them, and re-layouts: 1.32 us -> none  [body(): return (target, grads[:dim], grads[dim:])]
    pallas_call x1 -> x2, Pallas kernels: 4.9 us -> 5.58 us  [the longest x1 4.86 us: body(): pl.pallas_call(functools.partial(kernel, own), out_shape=(f32(1, group, o...]
  transfers between devices with their start and end apart: 2 -> 2, of which waited for: 2 -> 2; matrix products, arithmetic and copies ran while one was open for 3% -> 2% of each run, Pallas kernels for 5% -> 5%
where the time goes in v4:
time: 103 us; the launch traced here: 101 us
  blocking collectives  52.1 us (51%)
  waiting for transfers between devices  17.9 us (17%)
  starting transfers between devices  15.1 us (15%)
  Pallas kernels  10.7 us (10%)
  local copies, waits for them, and re-layouts  3.57 us (3%)
  other arithmetic  1.28 us (1%)
    all_to_all x1, blocking collectives, body(): lax.all_to_all(jnp.broadcast_to(share[None], (rest, piece, width)), REST,...  19.9 us
    all_to_all x1, blocking collectives, body(): lax.all_to_all(grads.reshape(parts, piece, width), SCATTER, 0, 0, tiled=T...  17.7 us
    all_to_all x1, blocking collectives, body(): lax.all_to_all(jnp.broadcast_to(share[None], (parts, piece, width)), SCAT...  14.4 us
    all_to_all x1, starting transfers between devices, body(): lax.all_to_all(jnp.broadcast_to(key_own[None], (peers, toks, dim)), CTX,...  13.2 us
    all_to_all x1, waiting for transfers between devices, body(): lax.all_to_all(jnp.broadcast_to(key_own[None], (peers, toks, dim)), CTX,...  12 us
    ppermute x1, waiting for transfers between devices, body(): far = lax.ppermute(near, ('y', 'c'), pairs)  5.89 us
    pallas_call x1, Pallas kernels, body(): pl.pallas_call(functools.partial(kernel, own), out_shape=(f32(1, group, o...  4.86 us
    pallas_call x1, Pallas kernels, body(): pl.pallas_call(functools.partial(half_kernel, own), out_shape=(f32(8, row...  3.32 us
  transfers between devices with their start and end apart: 2, of which 2 were waited for; matrix products, arithmetic and copies ran while one was open for 2% of the time, Pallas kernels for 5%

profile of v4, /device:TPU:1, one launch (start us, length us, event | category | flops | bytes accessed | tf_op | source)
XLA Modules:
  0.0 101.3 jit_solution(14072685466259535471)
XLA Ops:
  0.6 1.7 %broadcast_in_dim.26 = bf16[16,128,128]{2,1,0:T(8,128)(2,1)} broadcast(bf16[128,128]{1,0:T(8,128)(2,1)} %bitcast.18), dimensions={1,2} | broadcast | bytes 557056 | tf_op jit(solution)/shard_map/broadcast_in_dim | solution.py:264
  2.3 13.2 %all-to-all-start = ((bf16[16,128,128]{2,1,0:T(8,128)(2,1)}), bf16[16,128,128]{2,1,0:T(8,128)(2,1)S(1)}, u32[]{:S(2)}, u32[]{:S(2)}) async-start(bf16[16,128,128]{2,1,0:T(8,128)(2,1)} %broadcast_in_dim.26), calls=%async_computation | async-start | bytes 1048576 | tf_op jit(solution)/shard_map/all_to_all | solution.py:263
  15.5 0.0 copy-start
  15.5 0.6 copy-done
  16.1 0.0 copy-start.1
  16.1 0.1 dynamic_slice.8
  16.2 0.6 copy-done.1
  16.8 0.6 dynamic_slice.7
  17.4 1.8 %own_block.1 = (f32[1,640]{1,0:T(1,128)}, f32[8,640]{1,0:T(8,128)}, f32[16,128]{1,0:T(8,128)}, f32[16,128]{1,0:T(8,128)}) custom-call(bf16[640,128]{1,0:T(8,128)(2,1)} %bitcast.14, bf16[128,128]{1,0:T(8,128)(2,1)} %bitcast.19, f32[128,128]{1,0:T(8,128)} %wq.1), custom_call_target="tpu_custom_call" | custom-call | tf_op jit(solution)/shard_map/own_block/pallas_call | solution.py:277
  19.2 1.2 %pad_add_fusion.scal = s32[4]{0:T(128)} fusion(s32[1]{0:T(128)} %bitcast.2, s32[2]{0:T(128)S(1)} %dynamic_slice.8, s32[1]{0:T(128)} %dynamic_slice.7), kind=kLoop, calls=%fused_computation | loop fusion | flops 8 | bytes 32 | tf_op jit(solution)/shard_map/concatenate | solution.py:269
  20.4 12.0 %all-to-all-done = bf16[16,128,128]{2,1,0:T(8,128)(2,1)S(1)} async-done(((bf16[16,128,128]{2,1,0:T(8,128)(2,1)}), bf16[16,128,128]{2,1,0:T(8,128)(2,1)S(1)}, u32[]{:S(2)}, u32[]{:S(2)}) %all-to-all-start) | async-done | bytes 524320 | tf_op jit(solution)/shard_map/all_to_all | solution.py:263
  32.4 1.9 %collective-permute-start = (bf16[2048,128]{1,0:T(8,128)(2,1)S(1)}, bf16[2048,128]{1,0:T(8,128)(2,1)S(1)}, u32[]{:S(2)}, u32[]{:S(2)}) collective-permute-start(bf16[2048,128]{1,0:T(8,128)(2,1)S(1)} %bitcast.11), channel_id=1, source_target_pairs={{0,64},{1,449},{64,0},{65,129},{128,192},{129,65},{192,128},{193,2... | collective-permute-start | bytes 1572872 | tf_op jit(solution)/shard_map/ppermute | solution.py:291
  34.3 3.3 %teacher_near.1 = (f32[8,640]{1,0:T(8,128)}, f32[8,640]{1,0:T(8,128)}, f32[64,640]{1,0:T(8,128)}, f32[64,384]{1,0:T(8,128)}) custom-call(s32[4]{0:T(128)} %pad_add_fusion.scal, s32[64]{0:T(128)} %order.3, bf16[640,128]{1,0:T(8,128)(2,1)} %bitcast.15, bf16[2048,128]{1,0:T(8,128)(2,1)S(1)} %bitcast.12, f32[1,640]{1,0:T(1,128)} %get-tuple-element.27.high_ref.diag_ref, ...), custom_call_target="tpu_custom_call" | custom-call | tf_op jit(solution)/shard_map/teacher_near/pallas_call | solution.py:293
  37.6 5.9 %collective-permute-done.k_ref = bf16[2048,128]{1,0:T(8,128)(2,1)S(1)} collective-permute-done((bf16[2048,128]{1,0:T(8,128)(2,1)S(1)}, bf16[2048,128]{1,0:T(8,128)(2,1)S(1)}, u32[]{:S(2)}, u32[]{:S(2)}) %collective-permute-start) | collective-permute-done | bytes 524320 | tf_op jit(solution)/shard_map/ppermute | solution.py:291
  43.5 4.9 %teacher_gate.1 = (f32[1,5,2,64]{3,2,1,0:T(2,128)}, f32[512,128]{1,0:T(8,128)}) custom-call(s32[4]{0:T(128)} %pad_add_fusion.scal, s32[64]{0:T(128)} %order.3, bf16[640,128]{1,0:T(8,128)(2,1)} %bitcast.16, bf16[2048,128]{1,0:T(8,128)(2,1)S(1)} %collective-permute-done.k_ref, s32[1,64]{1,0:T(1,128)} %bitcast.20, ...), custom_call_target="tpu_custom_call" | custom-call | tf_op jit(solution)/shard_map/teacher_gate/pallas_call | solution.py:301
  48.4 17.7 %all_to_all.20 = f32[32,16,128]{2,1,0:T(8,128)S(1)} all-to-all(f32[32,16,128]{2,1,0:T(8,128)} %bitcast.17), channel_id=1, replica_groups=mesh['y'=8,'zl'=4,'x'=4,'zh'=2,'c'=2] {'x','y'}, dimensions={0} | all-to-all | bytes 524288 | tf_op jit(solution)/shard_map/all_to_all | solution.py:321
  66.1 19.9 %all_to_all.21 = f32[16,16,128]{2,1,0:T(8,128)S(1)} all-to-all(f32[16,16,128]{2,1,0:T(8,128)S(1)} %broadcast_in_dim.29), channel_id=1, replica_groups=mesh['y'=8,'zl'=4,'x'=4,'zh'=2,'c'=2] {'zh','zl','c'}, dimensions={0} | all-to-all | bytes 262144 | tf_op jit(solution)/shard_map/all_to_all | solution.py:323
  86.1 14.4 %all_to_all.22 = f32[32,16,128]{2,1,0:T(8,128)S(1)} all-to-all(f32[32,16,128]{2,1,0:T(8,128)S(1)} %broadcast_in_dim.30), channel_id=1, replica_groups=mesh['y'=8,'zl'=4,'x'=4,'zh'=2,'c'=2] {'x','y'}, dimensions={0} | all-to-all | bytes 524288 | tf_op jit(solution)/shard_map/all_to_all | solution.py:327
  100.6 0.7 split_grads.1
  (4 shorter events, 0.1 us)
Async XLA Ops:
  2.3 30.1 %all-to-all-start = ((bf16[16,128,128]{2,1,0:T(8,128)(2,1)}), bf16[16,128,128]{2,1,0:T(8,128)(2,1)S(1)}, u32[]{:S(2)}, u32[]{:S(2)}) async-start(bf16[16,128,128]{2,1,0:T(8,128)(2,1)} %broadcast_in_dim.26), calls=%async_computation | async-start | bytes 1048576 | tf_op jit(solution)/shard_map/all_to_all | solution.py:263
  15.5 0.7 copy-start
  16.1 0.7 copy-start.1
  32.4 11.1 %collective-permute-start = (bf16[2048,128]{1,0:T(8,128)(2,1)S(1)}, bf16[2048,128]{1,0:T(8,128)(2,1)S(1)}, u32[]{:S(2)}, u32[]{:S(2)}) collective-permute-start(bf16[2048,128]{1,0:T(8,128)(2,1)S(1)} %bitcast.11), channel_id=1, source_target_pairs={{0,64},{1,449},{64,0},{65,129},{128,192},{129,65},{192,128},{193,2... | collective-permute-start | bytes 1572872 | tf_op jit(solution)/shard_map/ppermute | solution.py:291

commit v5 on v4

--- a/solution.py
+++ b/solution.py
@@ -84,7 +84,7 @@
     return fold8(parts, op)
 
 
-def first_kernel(group, q_ref, k_ref, wq, high_ref, total_ref, pq_ref, xq_ref):
+def first_kernel(group, q_ref, k_ref, ord_ref, wq, high_ref, total_ref, ord_out, pq_ref, xq_ref):
     rows, dim = q_ref.shape
     toks = rows // group
     own = toks // BLK
@@ -102,10 +102,11 @@
     pq = jnp.sum(q.astype(jnp.float32).reshape(group * own, BLK, dim), axis=1) * (1.0 / BLK)
     pq = jnp.concatenate([pq, jnp.zeros((COUNT - group * own, dim), jnp.float32)], axis=0)
     pq_ref[...] = pq
+    ord_out[...] = ord_ref[...]
     xq_ref[...] = dot(pq, wq[...], ((1,), (0,)))
 
 
-def scan_keys(own, scal, order, odd, q, k_ref, diag, high, total, m_ref, pk_ref, s0, s1):
+def scan_keys(own, scal, order, odd, q, k_ref, diag, high, total, m_ref, pk_ref, s0, s1, before_last=None):
     rows, dim = q.shape
     toks = own * BLK
     scale = math.log2(math.e) / math.sqrt(dim)
@@ -156,6 +157,8 @@
     top = fill(0, s0)
     for c in range(chunks):
         ahead = fill(c + 1, bufs[(c + 1) % 2]) if c + 1 < chunks else None
+        if c + 1 == chunks and before_last is not None:
+            before_last()
         high, total = drain(c, bufs[c % 2], top, high, total)
         top = ahead
     return high, total
@@ -191,11 +194,33 @@
     part, pos = lane_part(rows, toks)
     block = lane_block(scal, part, own)
     m_ref[...] = jnp.full(m_ref.shape, MASKED, jnp.float32)
+    seen = lax.rem(lax.broadcasted_iota(jnp.int32, (blocks, 1), 0) // STEP, 2) == odd
+    row = lax.broadcasted_iota(jnp.int32, (COUNT, 1), 0)
+    qblock = lane_block(scal, lax.rem(row, own), own)
+    gate = {}
+
+    def gate_forward():
+        pq = pq_ref[...]
+        xq = xq_ref[...]
+        pk = jnp.where(seen, pk_in[...], pk_ref[...])
+        xk = dot(pk, wk[...], ((1,), (0,)))
+        rq = lax.rsqrt(jnp.mean(xq * xq, axis=1, keepdims=True) + EPS)
+        rk = lax.rsqrt(jnp.mean(xk * xk, axis=1, keepdims=True) + EPS)
+        uq = xq * rq
+        uk = xk * rk
+        gate_scale = 1.0 / math.sqrt(xq.shape[1])
+        logits = dot(uq, uk, ((1,), (1,))) * gate_scale
+        kblock = ordv[...]
+        allowed = (kblock <= qblock) & (kblock * BLK < length)
+        weights = jnp.where(allowed, jnp.exp(logits), 0.0)
+        soft = weights / jnp.sum(weights, axis=1, keepdims=True)
+        gate.update(pq=pq, pkt=jnp.transpose(pk), uq=uq, uk=uk, rq=rq, rk=rk, soft=soft)
+        gate.update(scale=gate_scale)
+
     high, total = scan_keys(
         own, scal, order, 1 - odd, q_ref[...], k_ref, diag_ref[...], high_ref[...],
-        total_ref[...], m_ref, pk_ref, s0, s1,
-    )
-    seen = lax.rem(lax.broadcasted_iota(jnp.int32, (blocks, 1), 0) // STEP, 2) == odd
+        total_ref[...], m_ref, pk_ref, s0, s1, gate_forward,
+    )
     m_ref[0:blocks, :] = jnp.where(seen, m_in[...], m_ref[0:blocks, :])
 
     log_total = jnp.log2(jnp.sum(total, axis=0, keepdims=True))
@@ -204,35 +229,20 @@
     pad = COUNT - group * own
     depth = jnp.concatenate([depth, jnp.full((pad, blocks), MASKED, jnp.float32)], axis=0)
     pooled = jnp.exp2(depth)
-    row = lax.broadcasted_iota(jnp.int32, (COUNT, 1), 0)
-    qblock = lane_block(scal, lax.rem(row, own), own)
     good = (qblock * BLK < length) & (row < group * own)
     totals = jnp.sum(pooled, axis=1, keepdims=True)
     target = jnp.where(good, pooled / jnp.where(good, totals, 1.0), 0.0)
     for h in range(group):
         t_ref[0, h] = target[own * h : own * (h + 1)]
 
-    pq = pq_ref[...]
-    xq = xq_ref[...]
-    pk = jnp.where(seen, pk_in[...], pk_ref[...])
-    xk = dot(pk, wk[...], ((1,), (0,)))
-    rq = lax.rsqrt(jnp.mean(xq * xq, axis=1, keepdims=True) + EPS)
-    rk = lax.rsqrt(jnp.mean(xk * xk, axis=1, keepdims=True) + EPS)
-    uq = xq * rq
-    uk = xk * rk
-    gate_scale = 1.0 / math.sqrt(xq.shape[1])
-    logits = dot(uq, uk, ((1,), (1,))) * gate_scale
-    kblock = ordv[...]
-    allowed = (kblock <= qblock) & (kblock * BLK < length)
-    weights = jnp.where(allowed, jnp.exp(logits), 0.0)
-    soft = weights / jnp.sum(weights, axis=1, keepdims=True)
-    dl = (soft * jnp.sum(target, axis=1, keepdims=True) - target) * gate_scale
+    dl = (gate["soft"] * jnp.sum(target, axis=1, keepdims=True) - target) * gate["scale"]
+    uq, uk, rq, rk = gate["uq"], gate["uk"], gate["rq"], gate["rk"]
     duq = dot(dl, uk, ((1,), (0,)))
     duk = dot(dl, uq, ((0,), (0,)))
     dxq = rq * (duq - uq * jnp.mean(duq * uq, axis=1, keepdims=True))
     dxk = rk * (duk - uk * jnp.mean(duk * uk, axis=1, keepdims=True))
-    g_ref[0:dim, :] = dot(pq, dxq, ((0,), (0,)))
-    g_ref[dim : 4 * dim, :] = dot(pk, dxk, ((0,), (0,)))
+    g_ref[0:dim, :] = dot(gate["pq"], dxq, ((0,), (0,)))
+    g_ref[dim : 4 * dim, :] = dot(gate["pkt"], dxk, ((1,), (0,)))
 
 
 def split_kernel(g_ref, q_ref, k_ref, sem):
@@ -240,6 +250,16 @@
     copies = [
         pltpu.make_async_copy(g_ref.at[pl.ds(0, rows)], q_ref, sem.at[0]),
         pltpu.make_async_copy(g_ref.at[pl.ds(rows, k_ref.shape[0])], k_ref, sem.at[1]),
+    ]
+    for copy in copies:
+        copy.start()
+    for copy in copies:
+        copy.wait()
+
+
+def repeat_kernel(x_ref, o_ref, sem):
+    copies = [
+        pltpu.make_async_copy(x_ref, o_ref.at[i], sem.at[i]) for i in range(o_ref.shape[0])
     ]
     for copy in copies:
         copy.start()
@@ -260,9 +280,17 @@
     odd = lax.rem(lax.axis_index("y"), 2)
     peers = ny // 2 * nz
     same = [[y * nz + z for y in range(h, ny, 2) for z in range(nz)] for h in range(2)]
+    anywhere = pl.BlockSpec(memory_space=pl.ANY)
+    repeated = pl.pallas_call(
+        repeat_kernel,
+        out_shape=jax.ShapeDtypeStruct((peers, toks, dim), key_own.dtype),
+        in_specs=[anywhere],
+        out_specs=anywhere,
+        scratch_shapes=[pltpu.SemaphoreType.DMA((peers,))],
+        name="repeat_keys",
+    )(key_own)
     near = lax.all_to_all(
-        jnp.broadcast_to(key_own[None], (peers, toks, dim)),
-        CTX, 0, 0, axis_index_groups=same, tiled=True,
+        repeated, CTX, 0, 0, axis_index_groups=same, tiled=True,
     ).reshape(peers * toks, dim)
     length = lax.dynamic_index_in_dim(conv_len, lax.axis_index(("zh", "c")))
     mine = lax.dynamic_slice_in_dim(block_order, lax.axis_index(CTX) * own, own)
@@ -274,15 +302,24 @@
     def f32(*shape):
         return jax.ShapeDtypeStruct(shape, jnp.float32)
 
+    def near_core(*shape):
+        return pltpu.VMEM(shape, jnp.float32)
+
+    def pinned(*arrays):
+        return [pltpu.with_memory_space_constraint(x, pltpu.VMEM) for x in arrays]
+
     first = pl.pallas_call(
         functools.partial(first_kernel, group),
-        out_shape=(f32(1, rows), f32(8, rows), f32(COUNT, dim), f32(COUNT, width)),
-        in_specs=[vmem] * 3,
-        out_specs=(vmem,) * 4,
+        out_shape=(
+            near_core(1, rows), near_core(8, rows), pltpu.VMEM((1, blocks), jnp.int32),
+            near_core(COUNT, dim), near_core(COUNT, width),
+        ),
+        in_specs=[vmem] * 4,
+        out_specs=(vmem,) * 5,
         name="own_block",
-    )(q, key_own, gate_wq)
+    )(q, key_own, block_order[None], gate_wq)
     near, scal, first = lax.optimization_barrier((near, scal, first))
-    high, total, pq, xq = first
+    high, total, ordv, pq, xq = first
     pairs = []
     for y in range(ny):
         for c in range(2):
@@ -292,15 +329,17 @@
     buffers = [pltpu.VMEM((STEP * BLK, rows), jnp.float32)] * 2
     after, total, m_half, pk_half = pl.pallas_call(
         functools.partial(half_kernel, own),
-        out_shape=(f32(8, rows), f32(8, rows), f32(blocks, rows), f32(blocks, 3 * dim)),
+        out_shape=(
+            near_core(8, rows), near_core(8, rows), near_core(blocks, rows), near_core(blocks, 3 * dim)
+        ),
         in_specs=[smem, smem] + [vmem] * 4,
         out_specs=(vmem,) * 4,
         scratch_shapes=buffers,
         name="teacher_near",
-    )(scal, block_order, q, pltpu.with_memory_space_constraint(near, pltpu.VMEM), high, total)
+    )(scal, block_order, *pinned(q, near, high, total))
     target, grads = pl.pallas_call(
         functools.partial(kernel, own),
-        out_shape=(f32(1, group, own, blocks), f32(4 * dim, width)),
+        out_shape=(f32(1, group, own, blocks), near_core(4 * dim, width)),
         in_specs=[smem, smem] + [vmem] * 11,
         out_specs=(vmem, vmem),
         scratch_shapes=[
@@ -310,9 +349,10 @@
         ],
         name="teacher_gate",
     )(
-        scal, block_order, q, pltpu.with_memory_space_constraint(far, pltpu.VMEM),
-        block_order[None], high, after, total, m_half, pk_half,
-        pq, xq, gate_wk,
+        scal, block_order,
+        *pinned(
+            q, far, ordv, high, after, total, m_half, pk_half, pq, xq, gate_wk
+        ),
     )
 
     parts = lax.axis_size(SCATTER)
@@ -327,7 +367,6 @@
     grads = lax.all_to_all(
         jnp.broadcast_to(share[None], (parts, piece, width)), SCATTER, 0, 0, tiled=True
     ).reshape(4 * dim, width)
-    anywhere = pl.BlockSpec(memory_space=pl.ANY)
     grad_wq, grad_wk = pl.pallas_call(
         split_kernel,
         out_shape=(f32(dim, width), f32(3 * dim, width)),
@@ -335,7 +374,7 @@
         out_specs=(anywhere, anywhere),
         scratch_shapes=[pltpu.SemaphoreType.DMA((2,))],
         name="split_grads",
-    )(pltpu.with_memory_space_constraint(grads, pltpu.VMEM))
+    )(*pinned(grads))
     return target, grad_wq, grad_wk
 
 

time: 103 us -> 117 us (1.14)
  Pallas kernels: 10.7 us -> 25 us
  local copies, waits for them, and re-layouts: 3.57 us -> 1.32 us
  waiting for transfers between devices: 17.9 us -> 20 us
    pallas_call x2 -> x3, Pallas kernels: 5.12 us -> 20.7 us  [the longest x1 17.1 us: body(): pl.pallas_call(repeat_kernel, out_shape=jax.ShapeDtypeStruct((peers, toks...]
    broadcast_in_dim x1 -> x0, local copies, waits for them, and re-layouts: 1.65 us -> none  [body(): jnp.broadcast_to(key_own[None], (peers, toks, dim))]
    pallas_call x1, Pallas kernels: 4.86 us -> 3.66 us  [body(): pl.pallas_call(functools.partial(kernel, own), out_shape=(f32(1, group, o...]
    all_to_all x1, waiting for transfers between devices: 12 us -> 13.1 us  [body(): lax.all_to_all(repeated, CTX, 0, 0, axis_index_groups=same, tiled=True)]
  transfers between devices with their start and end apart: 2 -> 2, of which waited for: 2 -> 2; matrix products, arithmetic and copies ran while one was open for 2% -> 2% of each run, Pallas kernels for 5% -> 3%
where the time goes in v5:
time: 117 us; the launch traced here: 115 us
  blocking collectives  51.9 us (44%)
  Pallas kernels  25 us (21%)
  waiting for transfers between devices  20 us (17%)
  starting transfers between devices  15.2 us (13%)
  local copies, waits for them, and re-layouts  1.32 us (1%)
  other arithmetic  1.29 us (1%)
    all_to_all x1, blocking collectives, body(): lax.all_to_all(jnp.broadcast_to(share[None], (rest, piece, width)), REST,...  19.9 us
    all_to_all x1, blocking collectives, body(): lax.all_to_all(grads.reshape(parts, piece, width), SCATTER, 0, 0, tiled=T...  17.5 us
    pallas_call x1, Pallas kernels, body(): pl.pallas_call(repeat_kernel, out_shape=jax.ShapeDtypeStruct((peers, toks...  17.1 us
    all_to_all x1, blocking collectives, body(): lax.all_to_all(jnp.broadcast_to(share[None], (parts, piece, width)), SCAT...  14.4 us
    all_to_all x1, starting transfers between devices, body(): lax.all_to_all(repeated, CTX, 0, 0, axis_index_groups=same, tiled=True)  13.2 us
    all_to_all x1, waiting for transfers between devices, body(): lax.all_to_all(repeated, CTX, 0, 0, axis_index_groups=same, tiled=True)  13.1 us
    ppermute x1, waiting for transfers between devices, body(): far = lax.ppermute(near, ('y', 'c'), pairs)  6.85 us
    pallas_call x1, Pallas kernels, body(): pl.pallas_call(functools.partial(kernel, own), out_shape=(f32(1, group, o...  3.66 us
  transfers between devices with their start and end apart: 2, of which 2 were waited for; matrix products, arithmetic and copies ran while one was open for 2% of the time, Pallas kernels for 3%

profile of v5, /device:TPU:1, one launch (start us, length us, event | category | flops | bytes accessed | tf_op | source)
XLA Modules:
  0.0 115.5 jit_solution(14222397051025943867)
XLA Ops:
  0.6 17.1 %repeat_keys.1 = bf16[16,128,128]{2,1,0:T(8,128)(2,1)} custom-call(bf16[128,128]{1,0:T(8,128)(2,1)} %bitcast.18), custom_call_target="tpu_custom_call" | custom-call | tf_op jit(solution)/shard_map/repeat_keys/pallas_call | solution.py:284
  17.8 13.2 %all-to-all-start = ((bf16[16,128,128]{2,1,0:T(8,128)(2,1)}), bf16[16,128,128]{2,1,0:T(8,128)(2,1)S(1)}, u32[]{:S(2)}, u32[]{:S(2)}) async-start(bf16[16,128,128]{2,1,0:T(8,128)(2,1)} %repeat_keys.1), calls=%async_computation | async-start | bytes 1048576 | tf_op jit(solution)/shard_map/all_to_all | solution.py:292
  31.0 0.0 copy-start.2
  31.0 0.0 copy-start.3
  31.0 0.0 copy-start
  31.0 0.6 copy-done.2
  31.6 0.1 dynamic_slice.8
  31.7 0.0 copy-done.3
  31.7 0.6 dynamic_slice.7
  32.3 1.2 %own_block.1 = (f32[1,640]{1,0:T(1,128)S(1)}, f32[8,640]{1,0:T(8,128)S(1)}, s32[1,64]{1,0:T(1,128)S(1)}, f32[16,128]{1,0:T(8,128)S(1)}, f32[16,128]{1,0:T(8,128)S(1)}) custom-call(bf16[640,128]{1,0:T(8,128)(2,1)} %bitcast.13, bf16[128,128]{1,0:T(8,128)(2,1)} %bitcast.19, s32[1,64]{1,0:T(1,128)} %bitcast.20, f32[128,128]{1,0:T(8,128)} %wq.1), custom_call_target="tpu_custom_call" | custom-call | tf_op jit(solution)/shard_map/own_block/pallas_call | solution.py:311
  33.5 1.2 %pad_add_fusion.scal = s32[4]{0:T(128)} fusion(s32[1]{0:T(128)} %bitcast.2, s32[2]{0:T(128)S(1)} %dynamic_slice.8, s32[1]{0:T(128)} %dynamic_slice.7), kind=kLoop, calls=%fused_computation | loop fusion | flops 8 | bytes 32 | tf_op jit(solution)/shard_map/concatenate | solution.py:297
  34.7 13.1 %all-to-all-done = bf16[16,128,128]{2,1,0:T(8,128)(2,1)S(1)} async-done(((bf16[16,128,128]{2,1,0:T(8,128)(2,1)}), bf16[16,128,128]{2,1,0:T(8,128)(2,1)S(1)}, u32[]{:S(2)}, u32[]{:S(2)}) %all-to-all-start) | async-done | bytes 524320 | tf_op jit(solution)/shard_map/all_to_all | solution.py:292
  47.9 0.0 copy-start.1
  47.9 2.0 %collective-permute-start = (bf16[2048,128]{1,0:T(8,128)(2,1)S(1)}, bf16[2048,128]{1,0:T(8,128)(2,1)S(1)}, u32[]{:S(2)}, u32[]{:S(2)}) collective-permute-start(bf16[2048,128]{1,0:T(8,128)(2,1)S(1)} %bitcast.11), channel_id=1, source_target_pairs={{0,64},{1,449},{64,0},{65,129},{128,192},{129,65},{192,128},{193,2... | collective-permute-start | bytes 1572872 | tf_op jit(solution)/shard_map/ppermute | solution.py:328
  49.9 0.0 copy-done
  49.9 2.3 %teacher_near.1 = (f32[8,640]{1,0:T(8,128)S(1)}, f32[8,640]{1,0:T(8,128)S(1)}, f32[64,640]{1,0:T(8,128)S(1)}, f32[64,384]{1,0:T(8,128)S(1)}) custom-call(s32[4]{0:T(128)} %pad_add_fusion.scal, s32[64]{0:T(128)} %order.3, bf16[640,128]{1,0:T(8,128)(2,1)S(1)} %bitcast.14, bf16[2048,128]{1,0:T(8,128)(2,1)S(1)} %bitcast.12, ...), custom_call_target="tpu_custom_call" | custom-call | tf_op jit(solution)/shard_map/teacher_near/pallas_call | solution.py:330
  52.3 6.9 %collective-permute-done.k_ref = bf16[2048,128]{1,0:T(8,128)(2,1)S(1)} collective-permute-done((bf16[2048,128]{1,0:T(8,128)(2,1)S(1)}, bf16[2048,128]{1,0:T(8,128)(2,1)S(1)}, u32[]{:S(2)}, u32[]{:S(2)}) %collective-permute-start) | collective-permute-done | bytes 524320 | tf_op jit(solution)/shard_map/ppermute | solution.py:328
  59.1 0.0 copy-done.1
  59.1 3.7 %teacher_gate.1 = (f32[1,5,2,64]{3,2,1,0:T(2,128)}, f32[512,128]{1,0:T(8,128)S(1)}) custom-call(s32[4]{0:T(128)} %pad_add_fusion.scal, s32[64]{0:T(128)} %order.3, bf16[640,128]{1,0:T(8,128)(2,1)S(1)} %bitcast.15, bf16[2048,128]{1,0:T(8,128)(2,1)S(1)} %collective-permute-done.k_ref, s32[1,64]{1,0:T(1,128)S(1)} %get-tuple-element.30.ordv, ...), custom_call_target="tpu_custom_call" | custom-call | tf_op jit(solution)/shard_map/teacher_gate/pallas_call | solution.py:340
  62.8 17.5 %all_to_all.20 = f32[32,16,128]{2,1,0:T(8,128)S(1)} all-to-all(f32[32,16,128]{2,1,0:T(8,128)S(1)} %bitcast.17), channel_id=1, replica_groups=mesh['y'=8,'zl'=4,'x'=4,'zh'=2,'c'=2] {'x','y'}, dimensions={0} | all-to-all | bytes 524288 | tf_op jit(solution)/shard_map/all_to_all | solution.py:361
  80.3 19.9 %all_to_all.21 = f32[16,16,128]{2,1,0:T(8,128)S(1)} all-to-all(f32[16,16,128]{2,1,0:T(8,128)S(1)} %broadcast_in_dim.20), channel_id=1, replica_groups=mesh['y'=8,'zl'=4,'x'=4,'zh'=2,'c'=2] {'zh','zl','c'}, dimensions={0} | all-to-all | bytes 262144 | tf_op jit(solution)/shard_map/all_to_all | solution.py:363
  100.3 14.4 %all_to_all.22 = f32[32,16,128]{2,1,0:T(8,128)S(1)} all-to-all(f32[32,16,128]{2,1,0:T(8,128)S(1)} %broadcast_in_dim.21), channel_id=1, replica_groups=mesh['y'=8,'zl'=4,'x'=4,'zh'=2,'c'=2] {'x','y'}, dimensions={0} | all-to-all | bytes 524288 | tf_op jit(solution)/shard_map/all_to_all | solution.py:367
  114.8 0.7 split_grads.1
  (4 shorter events, 0.1 us)
Async XLA Ops:
  17.8 30.1 %all-to-all-start = ((bf16[16,128,128]{2,1,0:T(8,128)(2,1)}), bf16[16,128,128]{2,1,0:T(8,128)(2,1)S(1)}, u32[]{:S(2)}, u32[]{:S(2)}) async-start(bf16[16,128,128]{2,1,0:T(8,128)(2,1)} %repeat_keys.1), calls=%async_computation | async-start | bytes 1048576 | tf_op jit(solution)/shard_map/all_to_all | solution.py:292
  31.0 0.7 copy-start.2
  31.0 0.7 copy-start.3
  31.0 18.9 %copy-start = (bf16[1,128,5,128]{3,1,2,0:T(8,128)(2,1)S(1)}, bf16[1,128,5,128]{3,1,2,0:T(8,128)(2,1)}, u32[]{:S(2)}) copy-start(bf16[1,128,5,128]{3,1,2,0:T(8,128)(2,1)} %param.6) | copy-start | bytes 491524
  47.9 11.3 %copy-start.1 = (f32[384,128]{1,0:T(8,128)S(1)}, f32[384,128]{1,0:T(8,128)}, u32[]{:S(2)}) copy-start(f32[384,128]{1,0:T(8,128)} %wk.1) | copy-start | bytes 589828
  47.9 11.3 %collective-permute-start = (bf16[2048,128]{1,0:T(8,128)(2,1)S(1)}, bf16[2048,128]{1,0:T(8,128)(2,1)S(1)}, u32[]{:S(2)}, u32[]{:S(2)}) collective-permute-start(bf16[2048,128]{1,0:T(8,128)(2,1)S(1)} %bitcast.11), channel_id=1, source_target_pairs={{0,64},{1,449},{64,0},{65,129},{128,192},{129,65},{192,128},{193,2... | collective-permute-start | bytes 1572872 | tf_op jit(solution)/shard_map/ppermute | solution.py:328

commit v6 on v5

--- a/solution.py
+++ b/solution.py
@@ -257,14 +257,8 @@
         copy.wait()
 
 
-def repeat_kernel(x_ref, o_ref, sem):
-    copies = [
-        pltpu.make_async_copy(x_ref, o_ref.at[i], sem.at[i]) for i in range(o_ref.shape[0])
-    ]
-    for copy in copies:
-        copy.start()
-    for copy in copies:
-        copy.wait()
+def repeat_kernel(x_ref, o_ref):
+    o_ref[...] = jnp.broadcast_to(x_ref[...][None], o_ref.shape)
 
 
 def body(queries, key_rows, block_order, conv_len, gate_wq, gate_wk):
@@ -280,13 +274,14 @@
     odd = lax.rem(lax.axis_index("y"), 2)
     peers = ny // 2 * nz
     same = [[y * nz + z for y in range(h, ny, 2) for z in range(nz)] for h in range(2)]
+    smem = pl.BlockSpec(memory_space=pltpu.SMEM)
+    vmem = pl.BlockSpec(memory_space=pltpu.VMEM)
     anywhere = pl.BlockSpec(memory_space=pl.ANY)
     repeated = pl.pallas_call(
         repeat_kernel,
-        out_shape=jax.ShapeDtypeStruct((peers, toks, dim), key_own.dtype),
-        in_specs=[anywhere],
-        out_specs=anywhere,
-        scratch_shapes=[pltpu.SemaphoreType.DMA((peers,))],
+        out_shape=pltpu.VMEM((peers, toks, dim), key_own.dtype),
+        in_specs=[vmem],
+        out_specs=vmem,
         name="repeat_keys",
     )(key_own)
     near = lax.all_to_all(
@@ -296,8 +291,6 @@
     mine = lax.dynamic_slice_in_dim(block_order, lax.axis_index(CTX) * own, own)
     scal = jnp.concatenate([length, mine, odd[None]])
     q = jnp.transpose(queries[0], (1, 0, 2)).reshape(rows, dim)
-    smem = pl.BlockSpec(memory_space=pltpu.SMEM)
-    vmem = pl.BlockSpec(memory_space=pltpu.VMEM)
 
     def f32(*shape):
         return jax.ShapeDtypeStruct(shape, jnp.float32)

time: 117 us -> 102 us (0.87)
  Pallas kernels: 25 us -> 9.55 us
    pallas_call x1, Pallas kernels: 17.1 us -> 1.65 us  [body(): pl.pallas_call(repeat_kernel, out_shape=pltpu.VMEM((peers, toks, dim), ke...]
  transfers between devices with their start and end apart: 2 -> 2, of which waited for: 2 -> 2; matrix products, arithmetic and copies ran while one was open for 2% -> 2% of each run, Pallas kernels for 3% -> 4%
where the time goes in v6:
time: 102 us; the launch traced here: 100 us
  blocking collectives  51.9 us (51%)
  waiting for transfers between devices  20 us (20%)
  starting transfers between devices  15.2 us (15%)
  Pallas kernels  9.55 us (9%)
  local copies, waits for them, and re-layouts  1.32 us (1%)
  other arithmetic  1.29 us (1%)
    all_to_all x1, blocking collectives, body(): lax.all_to_all(jnp.broadcast_to(share[None], (rest, piece, width)), REST,...  19.9 us
    all_to_all x1, blocking collectives, body(): lax.all_to_all(grads.reshape(parts, piece, width), SCATTER, 0, 0, tiled=T...  17.5 us
    all_to_all x1, blocking collectives, body(): lax.all_to_all(jnp.broadcast_to(share[None], (parts, piece, width)), SCAT...  14.4 us
    all_to_all x1, starting transfers between devices, body(): lax.all_to_all(repeated, CTX, 0, 0, axis_index_groups=same, tiled=True)  13.2 us
    all_to_all x1, waiting for transfers between devices, body(): lax.all_to_all(repeated, CTX, 0, 0, axis_index_groups=same, tiled=True)  13.1 us
    ppermute x1, waiting for transfers between devices, body(): far = lax.ppermute(near, ('y', 'c'), pairs)  6.85 us
    pallas_call x1, Pallas kernels, body(): pl.pallas_call(functools.partial(kernel, own), out_shape=(f32(1, group, o...  3.63 us
    pallas_call x1, Pallas kernels, body(): pl.pallas_call(functools.partial(half_kernel, own), out_shape=(near_core(...  2.34 us
  transfers between devices with their start and end apart: 2, of which 2 were waited for; matrix products, arithmetic and copies ran while one was open for 2% of the time, Pallas kernels for 4%

profile of v6, /device:TPU:1, one launch (start us, length us, event | category | flops | bytes accessed | tf_op | source)
XLA Modules:
  0.0 100.0 jit_solution(5982888825250869925)
XLA Ops:
  0.6 1.6 %repeat_keys.1 = bf16[16,128,128]{2,1,0:T(8,128)(2,1)} custom-call(bf16[128,128]{1,0:T(8,128)(2,1)} %bitcast.18), custom_call_target="tpu_custom_call" | custom-call | tf_op jit(solution)/shard_map/repeat_keys/pallas_call | solution.py:280
  2.3 13.2 %all-to-all-start = ((bf16[16,128,128]{2,1,0:T(8,128)(2,1)}), bf16[16,128,128]{2,1,0:T(8,128)(2,1)S(1)}, u32[]{:S(2)}, u32[]{:S(2)}) async-start(bf16[16,128,128]{2,1,0:T(8,128)(2,1)} %repeat_keys.1), calls=%async_computation | async-start | bytes 1048576 | tf_op jit(solution)/shard_map/all_to_all | solution.py:287
  15.5 0.0 copy-start.2
  15.5 0.0 copy-start.3
  15.5 0.0 copy-start
  15.5 0.6 copy-done.2
  16.1 0.1 dynamic_slice.8
  16.2 0.0 copy-done.3
  16.2 0.6 dynamic_slice.7
  16.8 1.2 %own_block.1 = (f32[1,640]{1,0:T(1,128)S(1)}, f32[8,640]{1,0:T(8,128)S(1)}, s32[1,64]{1,0:T(1,128)S(1)}, f32[16,128]{1,0:T(8,128)S(1)}, f32[16,128]{1,0:T(8,128)S(1)}) custom-call(bf16[640,128]{1,0:T(8,128)(2,1)} %bitcast.13, bf16[128,128]{1,0:T(8,128)(2,1)} %bitcast.19, s32[1,64]{1,0:T(1,128)} %bitcast.20, f32[128,128]{1,0:T(8,128)} %wq.1), custom_call_target="tpu_custom_call" | custom-call | tf_op jit(solution)/shard_map/own_block/pallas_call | solution.py:304
  18.0 1.2 %pad_add_fusion.scal = s32[4]{0:T(128)} fusion(s32[1]{0:T(128)} %bitcast.2, s32[2]{0:T(128)S(1)} %dynamic_slice.8, s32[1]{0:T(128)} %dynamic_slice.7), kind=kLoop, calls=%fused_computation | loop fusion | flops 8 | bytes 32 | tf_op jit(solution)/shard_map/concatenate | solution.py:292
  19.2 13.1 %all-to-all-done = bf16[16,128,128]{2,1,0:T(8,128)(2,1)S(1)} async-done(((bf16[16,128,128]{2,1,0:T(8,128)(2,1)}), bf16[16,128,128]{2,1,0:T(8,128)(2,1)S(1)}, u32[]{:S(2)}, u32[]{:S(2)}) %all-to-all-start) | async-done | bytes 524320 | tf_op jit(solution)/shard_map/all_to_all | solution.py:287
  32.4 0.0 copy-start.1
  32.4 2.0 %collective-permute-start = (bf16[2048,128]{1,0:T(8,128)(2,1)S(1)}, bf16[2048,128]{1,0:T(8,128)(2,1)S(1)}, u32[]{:S(2)}, u32[]{:S(2)}) collective-permute-start(bf16[2048,128]{1,0:T(8,128)(2,1)S(1)} %bitcast.11), channel_id=1, source_target_pairs={{0,64},{1,449},{64,0},{65,129},{128,192},{129,65},{192,128},{193,2... | collective-permute-start | bytes 1572872 | tf_op jit(solution)/shard_map/ppermute | solution.py:321
  34.4 0.0 copy-done
  34.4 2.3 %teacher_near.1 = (f32[8,640]{1,0:T(8,128)S(1)}, f32[8,640]{1,0:T(8,128)S(1)}, f32[64,640]{1,0:T(8,128)S(1)}, f32[64,384]{1,0:T(8,128)S(1)}) custom-call(s32[4]{0:T(128)} %pad_add_fusion.scal, s32[64]{0:T(128)} %order.3, bf16[640,128]{1,0:T(8,128)(2,1)S(1)} %bitcast.14, bf16[2048,128]{1,0:T(8,128)(2,1)S(1)} %bitcast.12, ...), custom_call_target="tpu_custom_call" | custom-call | tf_op jit(solution)/shard_map/teacher_near/pallas_call | solution.py:323
  36.8 6.8 %collective-permute-done.k_ref = bf16[2048,128]{1,0:T(8,128)(2,1)S(1)} collective-permute-done((bf16[2048,128]{1,0:T(8,128)(2,1)S(1)}, bf16[2048,128]{1,0:T(8,128)(2,1)S(1)}, u32[]{:S(2)}, u32[]{:S(2)}) %collective-permute-start) | collective-permute-done | bytes 524320 | tf_op jit(solution)/shard_map/ppermute | solution.py:321
  43.6 0.0 copy-done.1
  43.6 3.6 %teacher_gate.1 = (f32[1,5,2,64]{3,2,1,0:T(2,128)}, f32[512,128]{1,0:T(8,128)S(1)}) custom-call(s32[4]{0:T(128)} %pad_add_fusion.scal, s32[64]{0:T(128)} %order.3, bf16[640,128]{1,0:T(8,128)(2,1)S(1)} %bitcast.15, bf16[2048,128]{1,0:T(8,128)(2,1)S(1)} %collective-permute-done.k_ref, s32[1,64]{1,0:T(1,128)S(1)} %get-tuple-element.30.ordv, ...), custom_call_target="tpu_custom_call" | custom-call | tf_op jit(solution)/shard_map/teacher_gate/pallas_call | solution.py:333
  47.3 17.5 %all_to_all.20 = f32[32,16,128]{2,1,0:T(8,128)S(1)} all-to-all(f32[32,16,128]{2,1,0:T(8,128)S(1)} %bitcast.17), channel_id=1, replica_groups=mesh['y'=8,'zl'=4,'x'=4,'zh'=2,'c'=2] {'x','y'}, dimensions={0} | all-to-all | bytes 524288 | tf_op jit(solution)/shard_map/all_to_all | solution.py:354
  64.8 19.9 %all_to_all.21 = f32[16,16,128]{2,1,0:T(8,128)S(1)} all-to-all(f32[16,16,128]{2,1,0:T(8,128)S(1)} %broadcast_in_dim.20), channel_id=1, replica_groups=mesh['y'=8,'zl'=4,'x'=4,'zh'=2,'c'=2] {'zh','zl','c'}, dimensions={0} | all-to-all | bytes 262144 | tf_op jit(solution)/shard_map/all_to_all | solution.py:356
  84.8 14.4 %all_to_all.22 = f32[32,16,128]{2,1,0:T(8,128)S(1)} all-to-all(f32[32,16,128]{2,1,0:T(8,128)S(1)} %broadcast_in_dim.21), channel_id=1, replica_groups=mesh['y'=8,'zl'=4,'x'=4,'zh'=2,'c'=2] {'x','y'}, dimensions={0} | all-to-all | bytes 524288 | tf_op jit(solution)/shard_map/all_to_all | solution.py:360
  99.3 0.7 split_grads.1
  (4 shorter events, 0.1 us)
Async XLA Ops:
  2.3 30.1 %all-to-all-start = ((bf16[16,128,128]{2,1,0:T(8,128)(2,1)}), bf16[16,128,128]{2,1,0:T(8,128)(2,1)S(1)}, u32[]{:S(2)}, u32[]{:S(2)}) async-start(bf16[16,128,128]{2,1,0:T(8,128)(2,1)} %repeat_keys.1), calls=%async_computation | async-start | bytes 1048576 | tf_op jit(solution)/shard_map/all_to_all | solution.py:287
  15.5 0.7 copy-start.2
  15.5 0.7 copy-start.3
  15.5 18.9 %copy-start = (bf16[1,128,5,128]{3,1,2,0:T(8,128)(2,1)S(1)}, bf16[1,128,5,128]{3,1,2,0:T(8,128)(2,1)}, u32[]{:S(2)}) copy-start(bf16[1,128,5,128]{3,1,2,0:T(8,128)(2,1)} %param.6) | copy-start | bytes 491524
  32.4 11.3 %copy-start.1 = (f32[384,128]{1,0:T(8,128)S(1)}, f32[384,128]{1,0:T(8,128)}, u32[]{:S(2)}) copy-start(f32[384,128]{1,0:T(8,128)} %wk.1) | copy-start | bytes 589828
  32.4 11.3 %collective-permute-start = (bf16[2048,128]{1,0:T(8,128)(2,1)S(1)}, bf16[2048,128]{1,0:T(8,128)(2,1)S(1)}, u32[]{:S(2)}, u32[]{:S(2)}) collective-permute-start(bf16[2048,128]{1,0:T(8,128)(2,1)S(1)} %bitcast.11), channel_id=1, source_target_pairs={{0,64},{1,449},{64,0},{65,129},{128,192},{129,65},{192,128},{193,2... | collective-permute-start | bytes 1572872 | tf_op jit(solution)/shard_map/ppermute | solution.py:321
